TPU v7x, 32 devices: a whole 2x2x4 slice. The times are simulated.
32 devices in a mesh: member: 2 (over x), gx: 4 (over z), gy: 4 (over y, core).
Axes of the slice: x: 2, y: 2, z: 4, core: 2. Of those that a mesh axis runs over, the one named last changes fastest.
Arguments:
- perturb: bfloat16 [4, 20, 192, 512], P('member', None, 'gx', 'gy'), may hold values from -6 to 6
- gradient: float32 [20, 192, 512], P(None, 'gx', 'gy'), may hold values from -6 to 6
- vertical_eigenmodes: float32 [20, 20], replicated, may hold values from -1.25 to 1.25
- rate_x: float32 [20], replicated, may hold values from 1 to 512, as said below
- rate_y: float32 [20], replicated, may hold values from 1 to 512, as said below
Outputs:
- increment: float32 [20, 192, 512], P(None, 'gx', 'gy')
Inputs may be any that keep to these rules, and one draw needn't show every extreme that they name: `rate_x`: one rate for each mode. `rate_y`: one rate for each mode.
All inputs are finite; a program needn't handle non-finite values.
Results may differ from a plain program's by a relative error of at most 0.0003.
Values sent between devices are 32-bit elements; how exact they have to be, the bound alone decides.
No kernel may reach another device: no remote copies, remote signals or barrier semaphores. Data moves between devices by JAX's collectives and lax.ppermute only.
A program may use at most 64 MiB of HBM per device.

v0:
```python
import functools

import jax
import jax.numpy as jnp
from jax import lax
from jax.experimental import pallas as pl
from jax.experimental.pallas import tpu as pltpu
from jax.sharding import PartitionSpec as P

F32 = jnp.float32
BF16 = jnp.bfloat16
VMEM = pltpu.VMEM
SMEM = pltpu.SMEM
ORDER = 4
LANES = 128
SUB = 8


def poly(d, n):
    if d == 0:
        return jnp.ones_like(n) if hasattr(n, "shape") else 1.0
    if d == 1:
        return n
    if d == 2:
        return n * (n + 1.0) * 0.5
    return n * (n + 1.0) * (n + 2.0) * (1.0 / 6.0)


def gain(z):
    series = jnp.ones_like(z)
    for k in range(12, 1, -1):
        series = 1.0 - z * series * (1.0 / k)
    return jnp.where(z < 1.0, z * series, 1.0 - jnp.exp(-z))


def split(a):
    high = a.astype(BF16)
    return high, (a - high.astype(F32)).astype(BF16)


def dot(a, b):
    return jnp.dot(a, b, preferred_element_type=F32)


def dot3(a, b):
    return dot(a[0], b[0]) + (dot(a[0], b[1]) + dot(a[1], b[0]))


def exact(a, b, contract=((1,), (0,))):
    return lax.dot_general(
        a, b, (contract, ((), ())), precision=lax.Precision.HIGHEST, preferred_element_type=F32
    )


def iota(shape, axis):
    return lax.broadcasted_iota(jnp.int32, shape, axis)


def column_of(row, pick, rows):
    n = row.shape[1]
    wide = jnp.broadcast_to(row, (rows, n))
    hit = iota((rows, n), 1) == pick(iota((rows, n), 0))
    return jnp.sum(jnp.where(hit, wide, 0.0), axis=1, keepdims=True)


def expanded(matrix, rows, cols):
    left = (iota((rows * SUB, rows), 0) // SUB == iota((rows * SUB, rows), 1)).astype(F32)
    right = (iota((cols, cols * SUB), 1) // SUB == iota((cols, cols * SUB), 0)).astype(F32)
    full = exact(exact(left, matrix), right)
    shape = (rows * SUB, cols * SUB)
    return jnp.where(iota(shape, 0) % SUB == iota(shape, 1) % SUB, full, 0.0)


def shifted(coefficients, states):
    out = []
    for a in range(ORDER):
        total = coefficients[0] * states[a]
        for c in range(a):
            total = total + coefficients[a - c] * states[c]
        out.append(total)
    return out


def power(z, steps):
    decay = jnp.exp(-z * float(steps))
    return [decay * poly(d, float(steps)) for d in range(ORDER)]


def section(r, states, value):
    out = []
    for s in states:
        value = r * s + value
        out.append(value)
    return tuple(out)


def project_kernel(blocks, extent, p_ref, g_ref, e_ref, rx_ref, proj_ref, msg_ref, hat_ref, w_ref, y_ref):
    members, levels, nx, ny = p_ref.shape
    modes = e_ref.shape[1]
    rows = members * modes
    place = lax.axis_index("gx")
    rate = rx_ref[...]

    for m in range(members):
        for l in range(levels):
            w_ref[pl.ds((m * levels + l) * nx, nx), :] = p_ref[m, l].astype(F32) * g_ref[l]

    z_rows = column_of(rate, lambda i: i // SUB, modes * SUB) * (1.0 / extent)
    g_rows = gain(z_rows)
    mix = split(expanded(e_ref[...].T, modes, levels) * (g_rows * g_rows) * (g_rows * g_rows))
    for t in range(nx // SUB):
        wide = jnp.concatenate(
            [
                jnp.concatenate(
                    [w_ref[pl.ds((m * levels + l) * nx + t * SUB, SUB), :] for l in range(levels)], 0
                )
                for m in range(members)
            ],
            1,
        )
        done = dot3(mix, split(wide))
        for m in range(members):
            for k in range(modes):
                proj_ref[pl.ds((m * modes + k) * nx + t * SUB, SUB), :] = done[
                    k * SUB : (k + 1) * SUB, m * ny : (m + 1) * ny
                ]

    z = column_of(rate, lambda i: i % modes, rows) * (1.0 / extent)
    g = gain(z)
    full = (rows, ny)
    r = jnp.broadcast_to(jnp.exp(-z), full)
    pass_gain = jnp.broadcast_to((g * g) * (g * g), full)
    zeros = (jnp.zeros(full, F32),) * ORDER

    def onward(x, states):
        states = section(r, states, proj_ref[pl.ds(x, rows, stride=nx), :])
        y_ref[pl.ds(pl.multiple_of(x * rows, SUB), rows), :] = states[-1] * pass_gain
        return states

    def backward(n, states):
        x = nx - 1 - n
        return section(r, states, y_ref[pl.ds(pl.multiple_of(x * rows, SUB), rows), :])

    ends = lax.fori_loop(0, nx, onward, zeros, unroll=8)
    starts = lax.fori_loop(0, nx, backward, zeros, unroll=8)

    ahead = (blocks - 1 - place) * nx
    span = (blocks - 1) * nx
    span = -(-span // LANES) * LANES
    n = iota((rows, span), 1).astype(F32) + 1.0
    inside = iota((rows, span), 1) < ahead
    weight = jnp.where(inside, jnp.exp(-z * (2.0 * n - 1.0)), 0.0) * ((g * g) * (g * g))
    sums = {}
    for a in range(ORDER):
        for b in range(a, ORDER):
            sums[a, b] = jnp.sum(weight * poly(a, n) * poly(b, n), axis=1, keepdims=True)
            sums[b, a] = sums[a, b]
    hat = [[sums[a, ORDER - 1 - b] for b in range(ORDER)] for a in range(ORDER)]
    lane = iota((rows, LANES), 1)
    packed = jnp.zeros((rows, LANES), F32)
    for a in range(ORDER):
        for b in range(ORDER):
            packed = jnp.where(lane == a * ORDER + b, hat[a][b], packed)
    hat_ref[...] = packed

    turned = [sum(hat[a][b] * ends[b] for b in range(ORDER)) for a in range(ORDER)]
    turned = shifted(power(z, nx), turned)
    leaving = [starts[a] + turned[a] for a in range(ORDER)]
    for d in range(1, blocks):
        to_right = ends if d == 1 else shifted(power(z, (d - 1) * nx), ends)
        hops = blocks - d
        to_left = leaving if hops == 1 else shifted(power(z, (hops - 1) * nx), leaving)
        for a in range(ORDER):
            msg_ref[d - 1, pl.ds(a * rows, rows), :] = jnp.where(
                place + d < blocks, to_right[a], to_left[a]
            )


def table_kernel(blocks, extent, extent_x, e_ref, rx_ref, ry_ref, ry_s, send_ref, dy_ref, fix_ref, lift_ref, p_ref):
    modes = e_ref.shape[1]
    ny = dy_ref.shape[1]
    place = lax.axis_index("gy")
    states = modes * ORDER

    spread = (iota((modes, LANES), 1) // ORDER == iota((modes, LANES), 0)).astype(F32)
    live = (iota((1, LANES), 1) < states).astype(F32)
    lift = exact(e_ref[...], spread)
    lift_ref[...] = jnp.concatenate([lift, lift], 1)
    z = exact(ry_ref[...], spread) * (1.0 / extent)
    zx = exact(rx_ref[...], spread) * (1.0 / extent_x)
    g = gain(z)
    gx = gain(zx)
    pass_gain = (g * g) * (g * g) * live
    scale = jnp.sqrt((2.0 - g) / jnp.where(live > 0, g, 1.0)) * jnp.sqrt(
        (2.0 - gx) / jnp.where(live > 0, gx, 1.0)
    )
    scale = scale * live
    square = (LANES, LANES)
    eye = iota(square, 0) == iota(square, 1)

    def to_column(row):
        return jnp.sum(jnp.where(eye, jnp.broadcast_to(row, square), 0.0), axis=1, keepdims=True)

    def pick(index, choices):
        out = choices[0]
        for k in range(1, len(choices)):
            out = jnp.where(index == k, choices[k], out)
        return out

    z_col = to_column(z)
    scale_col = to_column(scale)
    gain_col = to_column(pass_gain)
    same = iota(square, 0) // ORDER == iota(square, 1) // ORDER
    row_state = iota(square, 0) % ORDER
    lane_state = iota(square, 1) % ORDER

    def moved(steps):
        if steps == 0:
            return jnp.where(eye, 1.0, 0.0)
        decay = jnp.exp(-z * float(steps))
        up = lane_state - row_state
        by = pick(up, [poly(d, float(steps)) for d in range(ORDER)])
        return jnp.where(same & (up >= 0), decay * by, 0.0)

    ahead = (blocks - 1 - place) * ny
    span = (blocks - 1) * ny
    n = iota((LANES, span), 1).astype(F32) + 1.0
    state = iota((LANES, span), 0) % ORDER
    inside = iota((LANES, span), 1) < ahead
    polys = [poly(d, n) for d in range(ORDER)]
    first = jnp.where(inside, jnp.exp(-z_col * n), 0.0) * pick(state, polys[::-1])
    second = jnp.exp(-z_col * (n - 1.0)) * pick(state, polys)
    hat = jnp.where(same, exact(first, second, ((1,), (1,))), 0.0)

    j = iota((ny, LANES), 0).astype(F32)
    lanes = iota((ny, LANES), 1) % ORDER
    from_end = float(ny) - j
    st = jnp.exp(-z * (from_end - 1.0)) * pick(lanes, [poly(a, from_end) for a in range(ORDER)]) * live
    sbt = jnp.exp(-z * j) * pick(lanes, [poly(a, j + 1.0) for a in range(ORDER)]) * live
    c_n = float(ny) - iota((LANES, ny), 1).astype(F32)
    c_state = iota((LANES, ny), 0) % ORDER
    cbt = jnp.exp(-z_col * c_n) * pick(c_state, [poly(ORDER - 1 - a, c_n) for a in range(ORDER)])
    bent = exact(st, hat)

    gap = iota((ny, ny), 1) - iota((ny, ny), 0)
    distance = jnp.maximum(gap, 0).astype(F32)
    p_ref[...] = jnp.where(gap >= 0, poly(ORDER - 1, distance + 1.0), 0.0)
    group = iota((ny, LANES), 1) // ORDER
    seen = jnp.zeros((ny, LANES), F32)
    for k in range(modes):
        rate = ry_s[k] * (1.0 / extent)
        up = jnp.exp(distance * (-rate)) * p_ref[...]
        mine = group == k
        seen = seen + exact(up, jnp.where(mine, sbt, 0.0))
        core = exact(up, up, ((1,), (1,))) + exact(jnp.where(mine, bent, 0.0), cbt)
        total = jnp.max(jnp.where(iota((1, LANES), 1) // ORDER == k, pass_gain * pass_gain * scale, 0.0))
        dy_ref[k] = core * total

    leaving = (seen + exact(bent, moved(ny))) * (pass_gain * pass_gain)
    for d in range(1, blocks):
        ends = float(d * ny) - j
        to_right = jnp.exp(-z * (ends - 1.0)) * pick(lanes, [poly(a, ends) for a in range(ORDER)]) * pass_gain
        to_left = exact(leaving, moved((blocks - d - 1) * ny))
        send_ref[:, pl.ds((d - 1) * LANES, LANES)] = jnp.where(place + d < blocks, to_right, to_left)

    flip = same & (row_state + lane_state == ORDER - 1)
    turned = exact(jnp.where(flip, jnp.exp(-z_col), 0.0), seen, ((1,), (1,)))
    bent_on = exact(exact(moved(ny), hat), cbt)
    fix_ref[0:LANES, :] = (turned + bent_on) * (gain_col * scale_col)
    fix_ref[LANES : 2 * LANES, :] = cbt * scale_col


def x_kernel(blocks, blocks_y, extent, proj_ref, hat_ref, rx_ref, send_ref, *refs):
    got = refs[: blocks - 1]
    z_ref, msg_refs, y_ref = refs[blocks - 1], refs[blocks:-1], refs[-1]
    rows = hat_ref.shape[0]
    modes = rx_ref.shape[1]
    members = rows // modes
    ny = proj_ref.shape[1]
    nx = proj_ref.shape[0] // rows
    place = lax.axis_index("gx")
    full = (rows, ny)
    z = column_of(rx_ref[...], lambda i: i % modes, rows) * (1.0 / extent)
    g = gain(z)
    r = jnp.broadcast_to(jnp.exp(-z), full)
    pass_gain = jnp.broadcast_to((g * g) * (g * g), full)

    left, right = [], []
    for a in range(ORDER):
        e = jnp.zeros(full, F32)
        b = jnp.zeros(full, F32)
        for d in range(1, blocks):
            value = got[d - 1][pl.ds(a * rows, rows), :]
            e = e + jnp.where(place >= d, value, 0.0)
            b = b + jnp.where(place >= d, 0.0, value)
        left.append(e)
        right.append(b)

    def onward(x, states):
        states = section(r, states, proj_ref[pl.ds(x, rows, stride=nx), :])
        y_ref[pl.ds(pl.multiple_of(x * rows, SUB), rows), :] = states[-1] * pass_gain
        return states

    def backward(n, states):
        x = nx - 1 - n
        at = pl.ds(pl.multiple_of(x * rows, SUB), rows)
        states = section(r, states, y_ref[at, :])
        z_ref[at, :] = states[-1]
        return states

    ends = lax.fori_loop(0, nx, onward, tuple(left), unroll=8)
    hat = hat_ref[...]
    for a in range(ORDER):
        for b in range(ORDER):
            at = a * ORDER + b
            right[a] = right[a] + hat[:, at : at + 1] * ends[b]
    lax.fori_loop(0, nx, backward, tuple(right), unroll=8)

    send = send_ref[...]
    group = (iota(send.shape, 1) % LANES) // ORDER
    total = jnp.zeros((members * nx, send.shape[1]), F32)
    for k in range(modes):
        value = jnp.concatenate(
            [z_ref[pl.ds(m * modes + k, nx, stride=rows), :] for m in range(members)], 0
        )
        total = total + dot3(split(value), split(jnp.where(group == k, send, 0.0)))
    for d in range(blocks_y - 1):
        msg_refs[d][...] = total[:, d * LANES : (d + 1) * LANES]


def local_kernel(z_ref, dy_ref, e_ref, out_ref, f_ref):
    levels, modes = e_ref.shape
    members = out_ref.shape[0] // levels
    nx = out_ref.shape[1]
    ny = z_ref.shape[1]
    rows = members * modes
    for k in range(modes):
        value = jnp.concatenate(
            [z_ref[pl.ds(m * modes + k, nx, stride=rows), :] for m in range(members)], 0
        )
        done = dot3(split(value), split(dy_ref[k]))
        for m in range(members):
            f_ref[pl.ds((m * modes + k) * nx, nx), :] = done[m * nx : (m + 1) * nx]
    mix = split(expanded(e_ref[...], levels, modes))
    for t in range(nx // SUB):
        wide = jnp.concatenate(
            [
                jnp.concatenate(
                    [f_ref[pl.ds((m * modes + k) * nx + t * SUB, SUB), :] for k in range(modes)], 0
                )
                for m in range(members)
            ],
            1,
        )
        done = dot3(mix, split(wide))
        for m in range(members):
            for l in range(levels):
                out_ref[m * levels + l, pl.ds(t * SUB, SUB), :] = done[
                    l * SUB : (l + 1) * SUB, m * ny : (m + 1) * ny
                ]


def final_kernel(blocks, total_members, p_ref, base_ref, fix_ref, lift_ref, *refs):
    got, out_ref = refs[:-1], refs[-1]
    members, levels, nx, ny = p_ref.shape
    place = lax.axis_index("gy")
    left = jnp.zeros(got[0].shape, F32)
    right = jnp.zeros(got[0].shape, F32)
    for d in range(1, blocks):
        value = got[d - 1][...]
        left = left + jnp.where(place >= d, value, 0.0)
        right = right + jnp.where(place >= d, 0.0, value)
    enter = jnp.concatenate([left, right], 1)
    fix = split(fix_ref[...])
    share = 1.0 / (total_members - 1)
    for l in range(levels):
        add = dot3(split(enter * lift_ref[pl.ds(l, 1), :]), fix)
        out = jnp.zeros((nx, ny), F32)
        for m in range(members):
            out = out + p_ref[m, l].astype(F32) * (
                base_ref[m * levels + l] + add[m * nx : (m + 1) * nx]
            )
        out_ref[l] = out * share


def call(kernel, out, ins, scratch=(), smem=(), flops=0, name=None):
    spec = lambda i: pl.BlockSpec(memory_space=SMEM if i in smem else VMEM)
    nbytes = sum(a.size * a.dtype.itemsize for a in ins) + sum(
        a.size * a.dtype.itemsize for a in jax.tree.leaves(out)
    )
    return pl.pallas_call(
        kernel,
        out_shape=out,
        in_specs=[spec(i) for i in range(len(ins))],
        out_specs=jax.tree.map(lambda _: pl.BlockSpec(memory_space=VMEM), out),
        scratch_shapes=list(scratch),
        cost_estimate=pl.CostEstimate(flops=flops, bytes_accessed=nbytes, transcendentals=0),
        name=name,
    )(*ins)


def shape(*dims):
    return jax.ShapeDtypeStruct(dims, F32)


def turn(value, axis, distance):
    n = lax.axis_size(axis)
    return lax.ppermute(value, axis, [(i, (i + distance) % n) for i in range(n)])


def body(perturb, gradient, vertical_eigenmodes, rate_x, rate_y):
    members, levels, nx, ny = perturb.shape
    modes = vertical_eigenmodes.shape[1]
    rows = members * modes
    blocks_x, blocks_y = lax.axis_size("gx"), lax.axis_size("gy")
    extent_x, extent_y = nx * blocks_x, ny * blocks_y
    row_x, row_y = rate_x[None, :], rate_y[None, :]

    proj, messages, hat = call(
        functools.partial(project_kernel, blocks_x, extent_x),
        (shape(rows * nx, ny), shape(blocks_x - 1, ORDER * rows, ny), shape(rows, LANES)),
        (perturb, gradient, vertical_eigenmodes, row_x),
        scratch=(VMEM((members * levels * nx, ny), F32), VMEM((rows * nx, ny), F32)),
        flops=1 << 28,
        name="project",
    )
    got = [turn(messages[d - 1], "gx", d) for d in range(1, blocks_x)]
    send, local, fix, lift = call(
        functools.partial(table_kernel, blocks_y, extent_y, extent_x),
        (
            shape(ny, (blocks_y - 1) * LANES),
            shape(modes, ny, ny),
            shape(2 * LANES, ny),
            shape(levels, 2 * LANES),
        ),
        (vertical_eigenmodes, row_x, row_y, rate_y),
        scratch=(VMEM((ny, ny), F32),),
        smem=(3,),
        flops=1 << 30,
        name="tables",
    )
    outs = call(
        functools.partial(x_kernel, blocks_x, blocks_y, extent_x),
        tuple([shape(rows * nx, ny)] + [shape(members * nx, LANES)] * (blocks_y - 1)),
        (proj, hat, row_x, send, *got),
        scratch=(VMEM((rows * nx, ny), F32),),
        flops=1 << 28,
        name="along_x",
    )
    filtered, sent = outs[0], outs[1:]
    got = [turn(sent[d - 1], "gy", d) for d in range(1, blocks_y)]
    base = call(
        local_kernel,
        shape(members * levels, nx, ny),
        (filtered, local, vertical_eigenmodes),
        scratch=(VMEM((rows * nx, ny), F32),),
        flops=1 << 29,
        name="along_y",
    )
    partial = call(
        functools.partial(final_kernel, blocks_y, members * lax.axis_size("member")),
        shape(levels, nx, ny),
        (perturb, base, fix, lift, *got),
        flops=1 << 28,
        name="restore",
    )
    if lax.axis_size("member") == 2:
        return partial + turn(partial, "member", 1)
    return lax.psum(partial, "member")


def solution(mesh):
    return jax.shard_map(
        body,
        mesh=mesh,
        in_specs=(P("member", None, "gx", "gy"), P(None, "gx", "gy"), P(), P(), P()),
        out_specs=P(None, "gx", "gy"),
        check_vma=False,
    )
```

profile of v0, /device:TPU:0, one launch (start us, length us, event | category | flops | bytes accessed | tf_op | source)
XLA Modules:
  0.0 49.6 jit_solution(11695254232550506006)
XLA Ops:
  0.0 4.1 %project.1 = (f32[1920,128]{1,0:T(8,128)}, f32[3,160,128]{2,1,0:T(8,128)}, f32[40,128]{1,0:T(8,128)}) custom-call(bf16[2,20,48,128]{3,2,1,0:T(8,128)(2,1)} %p_ref.3, f32[20,48,128]{2,1,0:T(8,128)} %g_ref.1, f32[20,20]{1,0:T(8,128)} %e_ref.5, f32[1,20]{1,0:T(1,128)} %bitcast.8), custom_call_target="tpu_custom_call" | custom-call | flops 268435456 | bytes 2234000 | tf_op jit(solution)/shard_map/project/pallas_call | solution.py:391
  4.1 1.0 %slice_bitcast_fusion = (f32[160,128]{1,0:T(8,128)S(1)}, f32[160,128]{1,0:T(8,128)S(1)}, f32[160,128]{1,0:T(8,128)S(1)}) fusion(f32[3,160,128]{2,1,0:T(8,128)} %get-tuple-element.19), kind=kLoop, calls=%fused_computation | loop fusion | bytes 491520 | tf_op jit(solution)/shard_map/squeeze | solution.py:427
  5.1 5.1 %collective-permute-start.2 = (f32[160,128]{1,0:T(8,128)S(1)}, f32[160,128]{1,0:T(8,128)S(1)}, u32[]{:S(2)}, u32[]{:S(2)}) collective-permute-start(f32[160,128]{1,0:T(8,128)S(1)} %get-tuple-element.27), channel_id=1, source_target_pairs={{0,12},{4,0},{8,4},{12,8},{1,13},{5,1},{9,5},{13,9},{2,14},{6,2},{... | collective-permute-start | bytes 245768 | tf_op jit(solution)/shard_map/ppermute | solution.py:408
  10.2 0.0 collective-permute-start.1
  10.2 1.0 %collective-permute-start = (f32[160,128]{1,0:T(8,128)S(1)}, f32[160,128]{1,0:T(8,128)S(1)}, u32[]{:S(2)}, u32[]{:S(2)}) collective-permute-start(f32[160,128]{1,0:T(8,128)S(1)} %get-tuple-element.29), channel_id=1, source_target_pairs={{0,4},{4,8},{8,12},{12,0},{1,5},{5,9},{9,13},{13,1},{2,6},{6,10},{... | collective-permute-start | bytes 245768 | tf_op jit(solution)/shard_map/ppermute | solution.py:408
  11.2 7.9 %tables.1 = (f32[128,384]{1,0:T(8,128)}, f32[20,128,128]{2,1,0:T(8,128)}, f32[256,128]{1,0:T(8,128)}, f32[20,256]{1,0:T(8,128)}) custom-call(f32[20,20]{1,0:T(8,128)} %e_ref.5, f32[1,20]{1,0:T(1,128)} %bitcast.9, f32[1,20]{1,0:T(1,128)} %bitcast.11, f32[20]{0:T(128)} %ry_s.1), custom_call_target="tpu_custom_call" | custom-call | flops 1073741824 | bytes 1660720 | tf_op jit(solution)/shard_map/tables/pallas_call | solution.py:391
  19.1 0.0 collective-permute-done.2.refs_2_
  19.1 0.0 copy-start
  19.1 0.0 collective-permute-done.1.refs_1_
  19.1 0.0 copy-start.1
  19.1 0.0 collective-permute-done.refs_0_
  19.2 0.0 copy-start.2
  19.2 0.6 %copy-done = f32[160,128]{1,0:T(8,128)} copy-done((f32[160,128]{1,0:T(8,128)}, f32[160,128]{1,0:T(8,128)S(1)}, u32[]{:S(2)}) %copy-start) | copy-done | bytes 81944
  19.7 0.0 copy-done.1
  19.8 0.0 copy-done.2
  19.8 4.5 %along_x.1 = (f32[1920,128]{1,0:T(8,128)}, f32[96,128]{1,0:T(8,128)}, f32[96,128]{1,0:T(8,128)}, f32[96,128]{1,0:T(8,128)}) custom-call(f32[1920,128]{1,0:T(8,128)} %get-tuple-element.16.proj_ref, f32[40,128]{1,0:T(8,128)} %get-tuple-element.17.hat_ref, f32[1,20]{1,0:T(1,128)} %bitcast.10, f32[128,384]{1,0:T(8,128)} %get-tuple-element.18.send_ref, ...), custom_call_target="tpu_custom_call" | custom-call | flops 268435456 | bytes 2576464 | tf_op jit(solution)/shard_map/along_x/pallas_call | solution.py:391
  24.4 0.0 collective-permute-start.3
  24.4 1.5 %collective-permute-start.4 = (f32[96,128]{1,0:T(8,128)}, f32[96,128]{1,0:T(8,128)S(1)}, u32[]{:S(2)}, u32[]{:S(2)}) collective-permute-start(f32[96,128]{1,0:T(8,128)} %get-tuple-element.25), channel_id=1, source_target_pairs={{0,2},{1,3},{2,0},{3,1},{4,6},{5,7},{6,4},{7,5},{8,10},{9,11},{10,... | collective-permute-start | bytes 147464 | tf_op jit(solution)/shard_map/ppermute | solution.py:408
  25.9 1.5 %collective-permute-start.5 = (f32[96,128]{1,0:T(8,128)}, f32[96,128]{1,0:T(8,128)S(1)}, u32[]{:S(2)}, u32[]{:S(2)}) collective-permute-start(f32[96,128]{1,0:T(8,128)} %get-tuple-element.26), channel_id=1, source_target_pairs={{0,3},{1,0},{2,1},{3,2},{4,7},{5,4},{6,5},{7,6},{8,11},{9,8},{10,9... | collective-permute-start | bytes 147464 | tf_op jit(solution)/shard_map/ppermute | solution.py:408
  27.3 4.2 %along_y.1.base_ref = f32[40,48,128]{2,1,0:T(8,128)} custom-call(f32[1920,128]{1,0:T(8,128)} %get-tuple-element.20.z_ref, f32[20,128,128]{2,1,0:T(8,128)} %get-tuple-element.21.dy_ref, f32[20,20]{1,0:T(8,128)} %e_ref.5), custom_call_target="tpu_custom_call" | custom-call | flops 536870912 | bytes 3278400 | tf_op jit(solution)/shard_map/along_y/pallas_call | solution.py:391
  31.6 0.0 collective-permute-done.3.refs_0_
  31.6 0.0 collective-permute-done.4.refs_1_
  31.6 0.0 copy-start.4
  31.6 0.0 collective-permute-done.5.refs_2_
  31.6 0.0 copy-start.5
  31.6 0.6 %copy-done.3 = f32[96,128]{1,0:T(8,128)} copy-done((f32[96,128]{1,0:T(8,128)}, f32[96,128]{1,0:T(8,128)S(1)}, u32[]{:S(2)}) %copy-start.3) | copy-done | bytes 49176
  32.2 0.0 copy-done.4
  32.2 0.0 copy-done.5
  32.2 3.1 %restore.1 = f32[20,48,128]{2,1,0:T(8,128)} custom-call(bf16[2,20,48,128]{3,2,1,0:T(8,128)(2,1)} %p_ref.3, f32[40,48,128]{2,1,0:T(8,128)} %along_y.1.base_ref, f32[256,128]{1,0:T(8,128)} %get-tuple-element.22.fix_ref, f32[20,256]{1,0:T(8,128)} %get-tuple-element.23.lift_ref, f32[96,128]{1,0:T(8,128)} %copy-done.3, f32[96,128]{1,0:T(8,128)} %copy-done.4, ...), custom_call_target="tpu_custom_call" | custom-call | flops 268435456 | bytes 2265088 | tf_op jit(solution)/shard_map/restore/pallas_call | solution.py:391
  35.3 1.5 %collective-permute-start.6 = (f32[20,48,128]{2,1,0:T(8,128)}, f32[20,48,128]{2,1,0:T(8,128)S(1)}, u32[]{:S(2)}, u32[]{:S(2)}) collective-permute-start(f32[20,48,128]{2,1,0:T(8,128)} %restore.1), channel_id=1, source_target_pairs={{0,16},{16,0},{1,17},{17,1},{2,18},{18,2},{3,19},{19,3},{4,20},{20... | collective-permute-start | bytes 1474568 | tf_op jit(solution)/shard_map/ppermute | solution.py:408
  36.8 10.9 %collective-permute-done.6 = f32[20,48,128]{2,1,0:T(8,128)S(1)} collective-permute-done((f32[20,48,128]{2,1,0:T(8,128)}, f32[20,48,128]{2,1,0:T(8,128)S(1)}, u32[]{:S(2)}, u32[]{:S(2)}) %collective-permute-start.6) | collective-permute-done | bytes 491552 | tf_op jit(solution)/shard_map/ppermute | solution.py:408
  47.7 1.9 %add.3 = f32[20,48,128]{2,1,0:T(8,128)} add(f32[20,48,128]{2,1,0:T(8,128)} %restore.1, f32[20,48,128]{2,1,0:T(8,128)S(1)} %collective-permute-done.6) | non-fusion elementwise | flops 122880 | bytes 1474560 | tf_op jit(solution)/shard_map/add | solution.py:468
  (1 shorter events, 0.0 us)
Async XLA Ops:
  5.1 14.1 %collective-permute-start.2 = (f32[160,128]{1,0:T(8,128)S(1)}, f32[160,128]{1,0:T(8,128)S(1)}, u32[]{:S(2)}, u32[]{:S(2)}) collective-permute-start(f32[160,128]{1,0:T(8,128)S(1)} %get-tuple-element.27), channel_id=1, source_target_pairs={{0,12},{4,0},{8,4},{12,8},{1,13},{5,1},{9,5},{13,9},{2,14},{6,2},{... | collective-permute-start | bytes 245768 | tf_op jit(solution)/shard_map/ppermute | solution.py:408
  10.2 8.9 %collective-permute-start.1 = (f32[160,128]{1,0:T(8,128)S(1)}, f32[160,128]{1,0:T(8,128)S(1)}, u32[]{:S(2)}, u32[]{:S(2)}) collective-permute-start(f32[160,128]{1,0:T(8,128)S(1)} %get-tuple-element.28), channel_id=1, source_target_pairs={{0,8},{4,12},{8,0},{12,4},{1,9},{5,13},{9,1},{13,5},{2,10},{6,14},... | collective-permute-start | bytes 245768 | tf_op jit(solution)/shard_map/ppermute | solution.py:408
  10.2 8.9 %collective-permute-start = (f32[160,128]{1,0:T(8,128)S(1)}, f32[160,128]{1,0:T(8,128)S(1)}, u32[]{:S(2)}, u32[]{:S(2)}) collective-permute-start(f32[160,128]{1,0:T(8,128)S(1)} %get-tuple-element.29), channel_id=1, source_target_pairs={{0,4},{4,8},{8,12},{12,0},{1,5},{5,9},{9,13},{13,1},{2,6},{6,10},{... | collective-permute-start | bytes 245768 | tf_op jit(solution)/shard_map/ppermute | solution.py:408
  19.1 0.6 %copy-start = (f32[160,128]{1,0:T(8,128)}, f32[160,128]{1,0:T(8,128)S(1)}, u32[]{:S(2)}) copy-start(f32[160,128]{1,0:T(8,128)S(1)} %collective-permute-done.2.refs_2_) | copy-start | bytes 245764
  19.1 0.7 %copy-start.1 = (f32[160,128]{1,0:T(8,128)}, f32[160,128]{1,0:T(8,128)S(1)}, u32[]{:S(2)}) copy-start(f32[160,128]{1,0:T(8,128)S(1)} %collective-permute-done.1.refs_1_) | copy-start | bytes 245764
  19.2 0.7 %copy-start.2 = (f32[160,128]{1,0:T(8,128)}, f32[160,128]{1,0:T(8,128)S(1)}, u32[]{:S(2)}) copy-start(f32[160,128]{1,0:T(8,128)S(1)} %collective-permute-done.refs_0_) | copy-start | bytes 245764
  24.4 7.2 %collective-permute-start.3 = (f32[96,128]{1,0:T(8,128)}, f32[96,128]{1,0:T(8,128)S(1)}, u32[]{:S(2)}, u32[]{:S(2)}) collective-permute-start(f32[96,128]{1,0:T(8,128)} %get-tuple-element.24), channel_id=1, source_target_pairs={{0,1},{1,2},{2,3},{3,0},{4,5},{5,6},{6,7},{7,4},{8,9},{9,10},{10,1... | collective-permute-start | bytes 147464 | tf_op jit(solution)/shard_map/ppermute | solution.py:408
  24.4 7.2 %collective-permute-start.4 = (f32[96,128]{1,0:T(8,128)}, f32[96,128]{1,0:T(8,128)S(1)}, u32[]{:S(2)}, u32[]{:S(2)}) collective-permute-start(f32[96,128]{1,0:T(8,128)} %get-tuple-element.25), channel_id=1, source_target_pairs={{0,2},{1,3},{2,0},{3,1},{4,6},{5,7},{6,4},{7,5},{8,10},{9,11},{10,... | collective-permute-start | bytes 147464 | tf_op jit(solution)/shard_map/ppermute | solution.py:408
  25.9 5.7 %collective-permute-start.5 = (f32[96,128]{1,0:T(8,128)}, f32[96,128]{1,0:T(8,128)S(1)}, u32[]{:S(2)}, u32[]{:S(2)}) collective-permute-start(f32[96,128]{1,0:T(8,128)} %get-tuple-element.26), channel_id=1, source_target_pairs={{0,3},{1,0},{2,1},{3,2},{4,7},{5,4},{6,5},{7,6},{8,11},{9,8},{10,9... | collective-permute-start | bytes 147464 | tf_op jit(solution)/shard_map/ppermute | solution.py:408
  31.6 0.6 %copy-start.3 = (f32[96,128]{1,0:T(8,128)}, f32[96,128]{1,0:T(8,128)S(1)}, u32[]{:S(2)}) copy-start(f32[96,128]{1,0:T(8,128)S(1)} %collective-permute-done.3.refs_0_) | copy-start | bytes 147460
  31.6 0.6 %copy-start.4 = (f32[96,128]{1,0:T(8,128)}, f32[96,128]{1,0:T(8,128)S(1)}, u32[]{:S(2)}) copy-start(f32[96,128]{1,0:T(8,128)S(1)} %collective-permute-done.4.refs_1_) | copy-start | bytes 147460
  31.6 0.6 %copy-start.5 = (f32[96,128]{1,0:T(8,128)}, f32[96,128]{1,0:T(8,128)S(1)}, u32[]{:S(2)}) copy-start(f32[96,128]{1,0:T(8,128)S(1)} %collective-permute-done.5.refs_2_) | copy-start | bytes 147460
  35.3 12.4 %collective-permute-start.6 = (f32[20,48,128]{2,1,0:T(8,128)}, f32[20,48,128]{2,1,0:T(8,128)S(1)}, u32[]{:S(2)}, u32[]{:S(2)}) collective-permute-start(f32[20,48,128]{2,1,0:T(8,128)} %restore.1), channel_id=1, source_target_pairs={{0,16},{16,0},{1,17},{17,1},{2,18},{18,2},{3,19},{19,3},{4,20},{20... | collective-permute-start | bytes 1474568 | tf_op jit(solution)/shard_map/ppermute | solution.py:408
where the time goes:
time: 50 us; the launch traced here: 49.6 us
  Pallas kernels  23.9 us (48%)
  waiting for transfers between devices  10.9 us (22%)
  starting transfers between devices  10.6 us (21%)
  local copies, waits for them, and re-layouts  2.27 us (5%)
  other arithmetic  1.88 us (4%)
    pallas_call x5, Pallas kernels, call(): pl.pallas_call(kernel, out_shape=out, in_specs=[spec(i) for i in range(le...  23.9 us
    ppermute x7, waiting for transfers between devices, turn(): lax.ppermute(value, axis, [(i, (i + distance) % n) for i in range(n)])  10.9 us
    ppermute x7, starting transfers between devices, turn(): lax.ppermute(value, axis, [(i, (i + distance) % n) for i in range(n)])  10.6 us
    add x1, other arithmetic, body(): return partial + turn(partial, 'member', 1)  1.88 us
    unnamed x12, local copies, waits for them, and re-layouts  1.29 us
  transfers between devices with their start and end apart: 7, of which 1 were waited for; matrix products, arithmetic and copies ran while one was open for 0% of the time, Pallas kernels for 24%

commit v1 on v0

--- a/solution.py
+++ b/solution.py
@@ -10,10 +10,10 @@
 F32 = jnp.float32
 BF16 = jnp.bfloat16
 VMEM = pltpu.VMEM
-SMEM = pltpu.SMEM
 ORDER = 4
 LANES = 128
 SUB = 8
+GRANT = 12 << 20
 
 
 def poly(d, n):
@@ -94,20 +94,31 @@
     return tuple(out)
 
 
-def project_kernel(blocks, extent, p_ref, g_ref, e_ref, rx_ref, proj_ref, msg_ref, hat_ref, w_ref, y_ref):
+def project_kernel(blocks, extent, p_hbm, g_hbm, e_hbm, rx_hbm, ry_hbm, proj_ref, hat_ref, e_ref, rx_ref, ry_ref, *refs):
+    msg_refs = refs[: blocks - 1]
+    p_ref, g_ref, w_ref, n_ref, y_ref, sems = refs[blocks - 1 :]
     members, levels, nx, ny = p_ref.shape
     modes = e_ref.shape[1]
     rows = members * modes
     place = lax.axis_index("gx")
+    pairs = [(e_hbm, e_ref), (rx_hbm, rx_ref), (ry_hbm, ry_ref), (g_hbm, g_ref)]
+    pairs = pairs + [(p_hbm.at[m], p_ref.at[m]) for m in range(members)]
+    copies = [pltpu.make_async_copy(a, b, sems.at[i]) for i, (a, b) in enumerate(pairs)]
+    for copy in copies:
+        copy.start()
+    for copy in copies[:3]:
+        copy.wait()
     rate = rx_ref[...]
 
+    z_rows = column_of(rate, lambda i: i // SUB, modes * SUB) * (1.0 / extent)
+    g_rows = gain(z_rows)
+    mix = split(expanded(e_ref[...].T, modes, levels) * (g_rows * g_rows) * (g_rows * g_rows))
+    for copy in copies[3:]:
+        copy.wait()
     for m in range(members):
         for l in range(levels):
             w_ref[pl.ds((m * levels + l) * nx, nx), :] = p_ref[m, l].astype(F32) * g_ref[l]
 
-    z_rows = column_of(rate, lambda i: i // SUB, modes * SUB) * (1.0 / extent)
-    g_rows = gain(z_rows)
-    mix = split(expanded(e_ref[...].T, modes, levels) * (g_rows * g_rows) * (g_rows * g_rows))
     for t in range(nx // SUB):
         wide = jnp.concatenate(
             [
@@ -121,7 +132,7 @@
         done = dot3(mix, split(wide))
         for m in range(members):
             for k in range(modes):
-                proj_ref[pl.ds((m * modes + k) * nx + t * SUB, SUB), :] = done[
+                n_ref[pl.ds((m * modes + k) * nx + t * SUB, SUB), :] = done[
                     k * SUB : (k + 1) * SUB, m * ny : (m + 1) * ny
                 ]
 
@@ -133,8 +144,11 @@
     zeros = (jnp.zeros(full, F32),) * ORDER
 
     def onward(x, states):
-        states = section(r, states, proj_ref[pl.ds(x, rows, stride=nx), :])
-        y_ref[pl.ds(pl.multiple_of(x * rows, SUB), rows), :] = states[-1] * pass_gain
+        at = pl.ds(pl.multiple_of(x * rows, SUB), rows)
+        value = n_ref[pl.ds(x, rows, stride=nx), :]
+        proj_ref[at, :] = value
+        states = section(r, states, value)
+        y_ref[at, :] = states[-1] * pass_gain
         return states
 
     def backward(n, states):
@@ -171,14 +185,14 @@
         hops = blocks - d
         to_left = leaving if hops == 1 else shifted(power(z, (hops - 1) * nx), leaving)
         for a in range(ORDER):
-            msg_ref[d - 1, pl.ds(a * rows, rows), :] = jnp.where(
+            msg_refs[d - 1][pl.ds(a * rows, rows), :] = jnp.where(
                 place + d < blocks, to_right[a], to_left[a]
             )
 
 
-def table_kernel(blocks, extent, extent_x, e_ref, rx_ref, ry_ref, ry_s, send_ref, dy_ref, fix_ref, lift_ref, p_ref):
+def table_kernel(blocks, extent, extent_x, e_ref, rx_ref, ry_ref, send_ref, high_ref, low_ref, fix_ref, lift_ref, own_ref, rise_ref, fall_ref):
     modes = e_ref.shape[1]
-    ny = dy_ref.shape[1]
+    ny = high_ref.shape[1]
     place = lax.axis_index("gy")
     states = modes * ORDER
 
@@ -241,27 +255,35 @@
     c_state = iota((LANES, ny), 0) % ORDER
     cbt = jnp.exp(-z_col * c_n) * pick(c_state, [poly(ORDER - 1 - a, c_n) for a in range(ORDER)])
     bent = exact(st, hat)
+    own_ref[...] = hat * pass_gain
 
     gap = iota((ny, ny), 1) - iota((ny, ny), 0)
-    distance = jnp.maximum(gap, 0).astype(F32)
-    p_ref[...] = jnp.where(gap >= 0, poly(ORDER - 1, distance + 1.0), 0.0)
+    rise = jnp.maximum(gap, 0).astype(F32)
+    fall = jnp.maximum(-gap, 0).astype(F32)
+    rise_ref[...] = jnp.where(gap >= 0, poly(ORDER - 1, rise + 1.0), 0.0)
+    fall_ref[...] = jnp.where(gap <= 0, poly(ORDER - 1, fall + 1.0), 0.0)
     group = iota((ny, LANES), 1) // ORDER
+    edge = split(sbt)
     seen = jnp.zeros((ny, LANES), F32)
     for k in range(modes):
-        rate = ry_s[k] * (1.0 / extent)
-        up = jnp.exp(distance * (-rate)) * p_ref[...]
-        mine = group == k
-        seen = seen + exact(up, jnp.where(mine, sbt, 0.0))
-        core = exact(up, up, ((1,), (1,))) + exact(jnp.where(mine, bent, 0.0), cbt)
-        total = jnp.max(jnp.where(iota((1, LANES), 1) // ORDER == k, pass_gain * pass_gain * scale, 0.0))
-        dy_ref[k] = core * total
+        rate = -z[:, k * ORDER : k * ORDER + 1]
+        up = split(jnp.exp(rise * rate) * rise_ref[...])
+        down = split(jnp.exp(fall * rate) * fall_ref[...])
+        both = dot3(up, [jnp.concatenate([down[i], edge[i]], 1) for i in range(2)])
+        high_ref[k], low_ref[k] = split(both[:, :ny])
+        seen = jnp.where(group == k, both[:, ny:], seen)
 
     leaving = (seen + exact(bent, moved(ny))) * (pass_gain * pass_gain)
+    wide = jnp.zeros(send_ref.shape, F32)
     for d in range(1, blocks):
         ends = float(d * ny) - j
         to_right = jnp.exp(-z * (ends - 1.0)) * pick(lanes, [poly(a, ends) for a in range(ORDER)]) * pass_gain
         to_left = exact(leaving, moved((blocks - d - 1) * ny))
-        send_ref[:, pl.ds((d - 1) * LANES, LANES)] = jnp.where(place + d < blocks, to_right, to_left)
+        chosen = jnp.where(place + d < blocks, to_right, to_left)
+        pad = jnp.zeros((ny, send_ref.shape[1] - LANES), F32)
+        chosen = jnp.concatenate([chosen, pad], 1) if pad.shape[1] else chosen
+        wide = wide + (pltpu.roll(chosen, (d - 1) * states, 1) if d > 1 else chosen)
+    send_ref[...] = wide
 
     flip = same & (row_state + lane_state == ORDER - 1)
     turned = exact(jnp.where(flip, jnp.exp(-z_col), 0.0), seen, ((1,), (1,)))
@@ -272,7 +294,7 @@
 
 def x_kernel(blocks, blocks_y, extent, proj_ref, hat_ref, rx_ref, send_ref, *refs):
     got = refs[: blocks - 1]
-    z_ref, msg_refs, y_ref = refs[blocks - 1], refs[blocks:-1], refs[-1]
+    f_ref, msg_refs, y_ref, z_ref = refs[blocks - 1], refs[blocks:-2], refs[-2], refs[-1]
     rows = hat_ref.shape[0]
     modes = rx_ref.shape[1]
     members = rows // modes
@@ -297,8 +319,9 @@
         right.append(b)
 
     def onward(x, states):
-        states = section(r, states, proj_ref[pl.ds(x, rows, stride=nx), :])
-        y_ref[pl.ds(pl.multiple_of(x * rows, SUB), rows), :] = states[-1] * pass_gain
+        at = pl.ds(pl.multiple_of(x * rows, SUB), rows)
+        states = section(r, states, proj_ref[at, :])
+        y_ref[at, :] = states[-1] * pass_gain
         return states
 
     def backward(n, states):
@@ -316,37 +339,41 @@
             right[a] = right[a] + hat[:, at : at + 1] * ends[b]
     lax.fori_loop(0, nx, backward, tuple(right), unroll=8)
 
-    send = send_ref[...]
-    group = (iota(send.shape, 1) % LANES) // ORDER
-    total = jnp.zeros((members * nx, send.shape[1]), F32)
     for k in range(modes):
-        value = jnp.concatenate(
-            [z_ref[pl.ds(m * modes + k, nx, stride=rows), :] for m in range(members)], 0
-        )
-        total = total + dot3(split(value), split(jnp.where(group == k, send, 0.0)))
+        for m in range(members):
+            f_ref[pl.ds((k * members + m) * nx, nx), :] = z_ref[pl.ds(m * modes + k, nx, stride=rows), :]
+    lines = members * nx
+    wide = dot3(split(f_ref[...]), split(send_ref[...]))
+    states = modes * ORDER
+    group = (iota((lines, wide.shape[1]), 1) % states) // ORDER
+    total = jnp.zeros(group.shape, F32)
+    for k in range(modes):
+        total = jnp.where(group == k, wide[k * lines : (k + 1) * lines], total)
     for d in range(blocks_y - 1):
-        msg_refs[d][...] = total[:, d * LANES : (d + 1) * LANES]
-
-
-def local_kernel(z_ref, dy_ref, e_ref, out_ref, f_ref):
+        moved = pltpu.roll(total, total.shape[1] - d * states, 1) if d else total
+        msg_refs[d][...] = moved[:, :LANES]
+
+
+def local_kernel(extent, extent_x, z_ref, high_ref, low_ref, e_ref, rx_ref, ry_ref, out_ref, f_ref):
     levels, modes = e_ref.shape
     members = out_ref.shape[0] // levels
     nx = out_ref.shape[1]
     ny = z_ref.shape[1]
-    rows = members * modes
+    lines = members * nx
     for k in range(modes):
-        value = jnp.concatenate(
-            [z_ref[pl.ds(m * modes + k, nx, stride=rows), :] for m in range(members)], 0
-        )
-        done = dot3(split(value), split(dy_ref[k]))
-        for m in range(members):
-            f_ref[pl.ds((m * modes + k) * nx, nx), :] = done[m * nx : (m + 1) * nx]
-    mix = split(expanded(e_ref[...], levels, modes))
+        high, low = split(z_ref[pl.ds(k * lines, lines), :])
+        wide = dot(high, jnp.concatenate([high_ref[k], low_ref[k]], 1))
+        f_ref[pl.ds(k * lines, lines), :] = wide[:, :ny] + (wide[:, ny:] + dot(low, high_ref[k]))
+    g = gain(ry_ref[...] * (1.0 / extent))
+    gx = gain(rx_ref[...] * (1.0 / extent_x))
+    pass_gain = (g * g) * (g * g)
+    scale = jnp.sqrt((2.0 - g) / g) * jnp.sqrt((2.0 - gx) / gx) * pass_gain * pass_gain
+    mix = split(expanded(e_ref[...] * scale, levels, modes))
     for t in range(nx // SUB):
         wide = jnp.concatenate(
             [
                 jnp.concatenate(
-                    [f_ref[pl.ds((m * modes + k) * nx + t * SUB, SUB), :] for k in range(modes)], 0
+                    [f_ref[pl.ds(k * lines + m * nx + t * SUB, SUB), :] for k in range(modes)], 0
                 )
                 for m in range(members)
             ],
@@ -360,12 +387,12 @@
                 ]
 
 
-def final_kernel(blocks, total_members, p_ref, base_ref, fix_ref, lift_ref, *refs):
+def final_kernel(blocks, total_members, p_ref, base_ref, fix_ref, lift_ref, own_ref, sent_ref, *refs):
     got, out_ref = refs[:-1], refs[-1]
     members, levels, nx, ny = p_ref.shape
     place = lax.axis_index("gy")
     left = jnp.zeros(got[0].shape, F32)
-    right = jnp.zeros(got[0].shape, F32)
+    right = exact(sent_ref[...], own_ref[...])
     for d in range(1, blocks):
         value = got[d - 1][...]
         left = left + jnp.where(place >= d, value, 0.0)
@@ -383,8 +410,8 @@
         out_ref[l] = out * share
 
 
-def call(kernel, out, ins, scratch=(), smem=(), flops=0, name=None):
-    spec = lambda i: pl.BlockSpec(memory_space=SMEM if i in smem else VMEM)
+def call(kernel, out, ins, scratch=(), far=False, flops=0, name=None):
+    spec = lambda i: pl.BlockSpec(memory_space=pltpu.HBM if far else VMEM)
     nbytes = sum(a.size * a.dtype.itemsize for a in ins) + sum(
         a.size * a.dtype.itemsize for a in jax.tree.leaves(out)
     )
@@ -395,6 +422,7 @@
         out_specs=jax.tree.map(lambda _: pl.BlockSpec(memory_space=VMEM), out),
         scratch_shapes=list(scratch),
         cost_estimate=pl.CostEstimate(flops=flops, bytes_accessed=nbytes, transcendentals=0),
+        compiler_params=pltpu.CompilerParams(vmem_limit_bytes=GRANT),
         name=name,
     )(*ins)
 
@@ -414,45 +442,53 @@
     rows = members * modes
     blocks_x, blocks_y = lax.axis_size("gx"), lax.axis_size("gy")
     extent_x, extent_y = nx * blocks_x, ny * blocks_y
-    row_x, row_y = rate_x[None, :], rate_y[None, :]
-
-    proj, messages, hat = call(
+
+    proj, hat, eigen, row_x, row_y, *messages = call(
         functools.partial(project_kernel, blocks_x, extent_x),
-        (shape(rows * nx, ny), shape(blocks_x - 1, ORDER * rows, ny), shape(rows, LANES)),
-        (perturb, gradient, vertical_eigenmodes, row_x),
-        scratch=(VMEM((members * levels * nx, ny), F32), VMEM((rows * nx, ny), F32)),
+        tuple(
+            [shape(rows * nx, ny), shape(rows, LANES), shape(levels, modes), shape(1, modes), shape(1, modes)]
+            + [shape(ORDER * rows, ny)] * (blocks_x - 1)
+        ),
+        tuple(
+            pltpu.with_memory_space_constraint(a, pltpu.HBM)
+            for a in (perturb, gradient, vertical_eigenmodes, rate_x[None, :], rate_y[None, :])
+        ),
+        scratch=(
+            VMEM(perturb.shape, perturb.dtype),
+            VMEM(gradient.shape, F32),
+            VMEM((members * levels * nx, ny), F32),
+            VMEM((rows * nx, ny), F32),
+            VMEM((rows * nx, ny), F32),
+            pltpu.SemaphoreType.DMA((4 + members,)),
+        ),
+        far=True,
         flops=1 << 28,
         name="project",
     )
     got = [turn(messages[d - 1], "gx", d) for d in range(1, blocks_x)]
-    send, local, fix, lift = call(
+    packed = -(-(blocks_y - 1) * modes * ORDER // LANES) * LANES
+    half = jax.ShapeDtypeStruct((modes, ny, ny), BF16)
+    send, high, low, fix, lift, own = call(
         functools.partial(table_kernel, blocks_y, extent_y, extent_x),
-        (
-            shape(ny, (blocks_y - 1) * LANES),
-            shape(modes, ny, ny),
-            shape(2 * LANES, ny),
-            shape(levels, 2 * LANES),
-        ),
-        (vertical_eigenmodes, row_x, row_y, rate_y),
-        scratch=(VMEM((ny, ny), F32),),
-        smem=(3,),
+        (shape(ny, packed), half, half, shape(2 * LANES, ny), shape(levels, 2 * LANES), shape(LANES, LANES)),
+        (eigen, row_x, row_y),
+        scratch=(VMEM((ny, ny), F32), VMEM((ny, ny), F32)),
         flops=1 << 30,
         name="tables",
     )
-    outs = call(
+    filtered, *sent = call(
         functools.partial(x_kernel, blocks_x, blocks_y, extent_x),
         tuple([shape(rows * nx, ny)] + [shape(members * nx, LANES)] * (blocks_y - 1)),
         (proj, hat, row_x, send, *got),
-        scratch=(VMEM((rows * nx, ny), F32),),
+        scratch=(VMEM((rows * nx, ny), F32), VMEM((rows * nx, ny), F32)),
         flops=1 << 28,
         name="along_x",
     )
-    filtered, sent = outs[0], outs[1:]
     got = [turn(sent[d - 1], "gy", d) for d in range(1, blocks_y)]
     base = call(
-        local_kernel,
+        functools.partial(local_kernel, extent_y, extent_x),
         shape(members * levels, nx, ny),
-        (filtered, local, vertical_eigenmodes),
+        (filtered, high, low, eigen, row_x, row_y),
         scratch=(VMEM((rows * nx, ny), F32),),
         flops=1 << 29,
         name="along_y",
@@ -460,7 +496,7 @@
     partial = call(
         functools.partial(final_kernel, blocks_y, members * lax.axis_size("member")),
         shape(levels, nx, ny),
-        (perturb, base, fix, lift, *got),
+        (perturb, base, fix, lift, own, sent[0], *got),
         flops=1 << 28,
         name="restore",
     )

time: 50 us -> 36.7 us (0.73)
  Pallas kernels: 23.9 us -> 10.6 us
  waiting for transfers between devices: 10.9 us -> 14.2 us
  local copies, waits for them, and re-layouts: 2.27 us -> 0.01 us
  other arithmetic: 1.88 us -> 0.84 us
    pallas_call x5, Pallas kernels: 23.9 us -> 10.6 us  [call(): pl.pallas_call(kernel, out_shape=out, in_specs=[spec(i) for i in range(le...]
    ppermute x7, waiting for transfers between devices: 10.9 us -> 14.2 us  [turn(): lax.ppermute(value, axis, [(i, (i + distance) % n) for i in range(n)])]
    unnamed x12 -> x2, local copies, waits for them, and re-layouts: 1.29 us -> 0.01 us
    add x1, other arithmetic: 1.88 us -> 0.84 us  [body(): return partial + turn(partial, 'member', 1)]
    squeeze x1 -> x0, local copies, waits for them, and re-layouts: 0.98 us -> none  [body(): got = [turn(messages[d - 1], 'gx', d) for d in range(1, blocks_x)]]
  transfers between devices with their start and end apart: 7 -> 7, of which waited for: 1 -> 6; matrix products, arithmetic and copies ran while one was open for 0% -> 0% of each run, Pallas kernels for 24% -> 12%
where the time goes in v1:
time: 36.7 us; the launch traced here: 36.5 us
  waiting for transfers between devices  14.2 us (39%)
  starting transfers between devices  10.7 us (29%)
  Pallas kernels  10.6 us (29%)
  other arithmetic  0.84 us (2%)
    ppermute x7, waiting for transfers between devices, turn(): lax.ppermute(value, axis, [(i, (i + distance) % n) for i in range(n)])  14.2 us
    ppermute x7, starting transfers between devices, turn(): lax.ppermute(value, axis, [(i, (i + distance) % n) for i in range(n)])  10.7 us
    pallas_call x5, Pallas kernels, call(): pl.pallas_call(kernel, out_shape=out, in_specs=[spec(i) for i in range(le...  10.6 us
    add x1, other arithmetic, body(): return partial + turn(partial, 'member', 1)  0.84 us
  transfers between devices with their start and end apart: 7, of which 6 were waited for; matrix products, arithmetic and copies ran while one was open for 0% of the time, Pallas kernels for 12%

profile of v1, /device:TPU:0, one launch (start us, length us, event | category | flops | bytes accessed | tf_op | source)
XLA Modules:
  0.0 36.5 jit_solution(9279852032225660116)
XLA Ops:
  0.0 2.9 %project.1 = (f32[1920,128]{1,0:T(8,128)S(1)}, f32[40,128]{1,0:T(8,128)S(1)}, f32[20,20]{1,0:T(8,128)S(1)}, f32[1,20]{1,0:T(1,128)S(1)}, f32[1,20]{1,0:T(1,128)S...) custom-call(bf16[2,20,48,128]{3,2,1,0:T(8,128)(2,1)} %p_ref.1, f32[20,48,128]{2,1,0:T(8,128)} %g_hbm.1, ...), custom_call_target="tpu_custom_call" | custom-call | flops 268435456 | bytes 2235840 | tf_op jit(solution)/shard_map/project/pallas_call | solution.py:418
  2.9 3.1 %collective-permute-start = (f32[160,128]{1,0:T(8,128)S(1)}, f32[160,128]{1,0:T(8,128)S(1)}, u32[]{:S(2)}, u32[]{:S(2)}) collective-permute-start(f32[160,128]{1,0:T(8,128)S(1)} %get-tuple-element.29), channel_id=1, source_target_pairs={{0,4},{4,8},{8,12},{12,0},{1,5},{5,9},{9,13},{13,1},{2,6},{6,10},{... | collective-permute-start | bytes 245768 | tf_op jit(solution)/shard_map/ppermute | solution.py:436
  6.0 2.6 %collective-permute-start.1 = (f32[160,128]{1,0:T(8,128)S(1)}, f32[160,128]{1,0:T(8,128)S(1)}, u32[]{:S(2)}, u32[]{:S(2)}) collective-permute-start(f32[160,128]{1,0:T(8,128)S(1)} %get-tuple-element.30), channel_id=1, source_target_pairs={{0,8},{4,12},{8,0},{12,4},{1,9},{5,13},{9,1},{13,5},{2,10},{6,14},... | collective-permute-start | bytes 245768 | tf_op jit(solution)/shard_map/ppermute | solution.py:436
  8.6 1.3 %collective-permute-start.2 = (f32[160,128]{1,0:T(8,128)S(1)}, f32[160,128]{1,0:T(8,128)S(1)}, u32[]{:S(2)}, u32[]{:S(2)}) collective-permute-start(f32[160,128]{1,0:T(8,128)S(1)} %get-tuple-element.31), channel_id=1, source_target_pairs={{0,12},{4,0},{8,4},{12,8},{1,13},{5,1},{9,5},{13,9},{2,14},{6,2},{... | collective-permute-start | bytes 245768 | tf_op jit(solution)/shard_map/ppermute | solution.py:436
  10.0 2.9 %tables.1 = (f32[128,256]{1,0:T(8,128)S(1)}, bf16[20,128,128]{2,1,0:T(8,128)(2,1)S(1)}, bf16[20,128,128]{2,1,0:T(8,128)(2,1)S(1)}, f32[256,128]{1,0:T(8,128)S(1)...) custom-call(f32[20,20]{1,0:T(8,128)S(1)} %get-tuple-element.26.e_ref, f32[1,20]{1,0:T(1,128)S(1)} %get-tuple-element.25.rx_ref, ...), custom_call_target="tpu_custom_call" | custom-call | flops 1073741824 | bytes 1660640 | tf_op jit(solution)/shard_map/tables/pallas_call | solution.py:418
  12.9 0.0 collective-permute-done.refs_0_
  12.9 1.2 %collective-permute-done.1.refs_1_ = f32[160,128]{1,0:T(8,128)S(1)} collective-permute-done((f32[160,128]{1,0:T(8,128)S(1)}, f32[160,128]{1,0:T(8,128)S(1)}, u32[]{:S(2)}, u32[]{:S(2)}) %collective-permute-start.1) | collective-permute-done | bytes 81952 | tf_op jit(solution)/shard_map/ppermute | solution.py:436
  14.1 0.2 collective-permute-done.2.refs_2_
  14.3 1.9 %along_x.1 = (f32[1920,128]{1,0:T(8,128)S(1)}, f32[96,128]{1,0:T(8,128)S(1)}, f32[96,128]{1,0:T(8,128)S(1)}, f32[96,128]{1,0:T(8,128)S(1)}) custom-call(f32[1920,128]{1,0:T(8,128)S(1)} %get-tuple-element.23.proj_ref, f32[40,128]{1,0:T(8,128)S(1)} %get-tuple-element.24.hat_ref, f32[1,20]{1,0:T(1,128)S(1)} %get-tuple-element.25.rx_ref, ...), custom_call_target="tpu_custom_call" | custom-call | flops 268435456 | bytes 2510928 | tf_op jit(solution)/shard_map/along_x/pallas_call | solution.py:418
  16.3 1.6 %collective-permute-start.4 = (f32[96,128]{1,0:T(8,128)S(1)}, f32[96,128]{1,0:T(8,128)S(1)}, u32[]{:S(2)}, u32[]{:S(2)}) collective-permute-start(f32[96,128]{1,0:T(8,128)S(1)} %get-tuple-element.39), channel_id=1, source_target_pairs={{0,2},{1,3},{2,0},{3,1},{4,6},{5,7},{6,4},{7,5},{8,10},{9,11},{10,... | collective-permute-start | bytes 147464 | tf_op jit(solution)/shard_map/ppermute | solution.py:436
  17.9 0.0 collective-permute-start.5
  17.9 0.5 %collective-permute-start.3 = (f32[96,128]{1,0:T(8,128)S(1)}, f32[96,128]{1,0:T(8,128)S(1)}, u32[]{:S(2)}, u32[]{:S(2)}) collective-permute-start(f32[96,128]{1,0:T(8,128)S(1)} %get-tuple-element.38.sent_ref), channel_id=1, source_target_pairs={{0,1},{1,2},{2,3},{3,0},{4,5},{5,6},{6,7},{7,4},{8,9},{9,10},{10,1... | collective-permute-start | bytes 147464 | tf_op jit(solution)/shard_map/ppermute | solution.py:436
  18.4 0.0 copy-start
  18.4 1.6 %along_y.1.base_ref = f32[40,48,128]{2,1,0:T(8,128)S(1)} custom-call(f32[1920,128]{1,0:T(8,128)S(1)} %get-tuple-element.32.z_ref, bf16[20,128,128]{2,1,0:T(8,128)(2,1)S(1)} %get-tuple-element.33.high_ref, bf16[20,128,128]{2,1,0:T(8,128)(2,1)S(1)} %get-tuple-element.34.low_ref, f32[20,20]{1,0:T(8,128)S(1)} %get-tuple-element.26.e_ref, ...), custom_call_target="tpu_custom_call" | custom-call | flops 536870912 | bytes 3278560 | tf_op jit(solution)/shard_map/along_y/pallas_call | solution.py:418
  20.1 0.4 %collective-permute-done.4.refs_1_ = f32[96,128]{1,0:T(8,128)S(1)} collective-permute-done((f32[96,128]{1,0:T(8,128)S(1)}, f32[96,128]{1,0:T(8,128)S(1)}, u32[]{:S(2)}, u32[]{:S(2)}) %collective-permute-start.4) | collective-permute-done | bytes 49184 | tf_op jit(solution)/shard_map/ppermute | solution.py:436
  20.5 0.1 collective-permute-done.5.refs_2_
  20.6 0.9 %collective-permute-done.3.refs_0_ = f32[96,128]{1,0:T(8,128)S(1)} collective-permute-done((f32[96,128]{1,0:T(8,128)S(1)}, f32[96,128]{1,0:T(8,128)S(1)}, u32[]{:S(2)}, u32[]{:S(2)}) %collective-permute-start.3) | collective-permute-done | bytes 49184 | tf_op jit(solution)/shard_map/ppermute | solution.py:436
  21.5 0.0 copy-done
  21.5 1.2 %restore.1 = f32[20,48,128]{2,1,0:T(8,128)S(1)} custom-call(bf16[2,20,48,128]{3,2,1,0:T(8,128)(2,1)S(1)} %copy-done, f32[40,48,128]{2,1,0:T(8,128)S(1)} %along_y.1.base_ref, f32[256,128]{1,0:T(8,128)S(1)} %get-tuple-element.35.fix_ref, f32[20,256]{1,0:T(8,128)S(1)} %get-tuple-element.36.lift_ref, f32[128,128]{1,0:T(8,128)S(1)} %get-tuple-element.37.own_ref, ...), custom_call_target="tpu_custom_call" | custom-call | flops 268435456 | bytes 2379776 | tf_op jit(solution)/shard_map/restore/pallas_call | solution.py:418
  22.7 1.6 %collective-permute-start.6 = (f32[20,48,128]{2,1,0:T(8,128)S(1)}, f32[20,48,128]{2,1,0:T(8,128)S(1)}, u32[]{:S(2)}, u32[]{:S(2)}) collective-permute-start(f32[20,48,128]{2,1,0:T(8,128)S(1)} %restore.1), channel_id=1, source_target_pairs={{0,16},{16,0},{1,17},{17,1},{2,18},{18,2},{3,19},{19,3},{4,20},{20... | collective-permute-start | bytes 1474568 | tf_op jit(solution)/shard_map/ppermute | solution.py:436
  24.3 11.3 %collective-permute-done.6 = f32[20,48,128]{2,1,0:T(8,128)S(1)} collective-permute-done((f32[20,48,128]{2,1,0:T(8,128)S(1)}, f32[20,48,128]{2,1,0:T(8,128)S(1)}, u32[]{:S(2)}, u32[]{:S(2)}) %collective-permute-start.6) | collective-permute-done | bytes 491552 | tf_op jit(solution)/shard_map/ppermute | solution.py:436
  35.6 0.8 %add.3 = f32[20,48,128]{2,1,0:T(8,128)} add(f32[20,48,128]{2,1,0:T(8,128)S(1)} %restore.1, f32[20,48,128]{2,1,0:T(8,128)S(1)} %collective-permute-done.6) | non-fusion elementwise | flops 122880 | bytes 1474560 | tf_op jit(solution)/shard_map/add | solution.py:504
Async XLA Ops:
  2.9 10.0 %collective-permute-start = (f32[160,128]{1,0:T(8,128)S(1)}, f32[160,128]{1,0:T(8,128)S(1)}, u32[]{:S(2)}, u32[]{:S(2)}) collective-permute-start(f32[160,128]{1,0:T(8,128)S(1)} %get-tuple-element.29), channel_id=1, source_target_pairs={{0,4},{4,8},{8,12},{12,0},{1,5},{5,9},{9,13},{13,1},{2,6},{6,10},{... | collective-permute-start | bytes 245768 | tf_op jit(solution)/shard_map/ppermute | solution.py:436
  6.0 8.1 %collective-permute-start.1 = (f32[160,128]{1,0:T(8,128)S(1)}, f32[160,128]{1,0:T(8,128)S(1)}, u32[]{:S(2)}, u32[]{:S(2)}) collective-permute-start(f32[160,128]{1,0:T(8,128)S(1)} %get-tuple-element.30), channel_id=1, source_target_pairs={{0,8},{4,12},{8,0},{12,4},{1,9},{5,13},{9,1},{13,5},{2,10},{6,14},... | collective-permute-start | bytes 245768 | tf_op jit(solution)/shard_map/ppermute | solution.py:436
  8.6 5.7 %collective-permute-start.2 = (f32[160,128]{1,0:T(8,128)S(1)}, f32[160,128]{1,0:T(8,128)S(1)}, u32[]{:S(2)}, u32[]{:S(2)}) collective-permute-start(f32[160,128]{1,0:T(8,128)S(1)} %get-tuple-element.31), channel_id=1, source_target_pairs={{0,12},{4,0},{8,4},{12,8},{1,13},{5,1},{9,5},{13,9},{2,14},{6,2},{... | collective-permute-start | bytes 245768 | tf_op jit(solution)/shard_map/ppermute | solution.py:436
  16.3 4.2 %collective-permute-start.4 = (f32[96,128]{1,0:T(8,128)S(1)}, f32[96,128]{1,0:T(8,128)S(1)}, u32[]{:S(2)}, u32[]{:S(2)}) collective-permute-start(f32[96,128]{1,0:T(8,128)S(1)} %get-tuple-element.39), channel_id=1, source_target_pairs={{0,2},{1,3},{2,0},{3,1},{4,6},{5,7},{6,4},{7,5},{8,10},{9,11},{10,... | collective-permute-start | bytes 147464 | tf_op jit(solution)/shard_map/ppermute | solution.py:436
  17.9 2.7 %collective-permute-start.5 = (f32[96,128]{1,0:T(8,128)S(1)}, f32[96,128]{1,0:T(8,128)S(1)}, u32[]{:S(2)}, u32[]{:S(2)}) collective-permute-start(f32[96,128]{1,0:T(8,128)S(1)} %get-tuple-element.40), channel_id=1, source_target_pairs={{0,3},{1,0},{2,1},{3,2},{4,7},{5,4},{6,5},{7,6},{8,11},{9,8},{10,9... | collective-permute-start | bytes 147464 | tf_op jit(solution)/shard_map/ppermute | solution.py:436
  17.9 3.6 %collective-permute-start.3 = (f32[96,128]{1,0:T(8,128)S(1)}, f32[96,128]{1,0:T(8,128)S(1)}, u32[]{:S(2)}, u32[]{:S(2)}) collective-permute-start(f32[96,128]{1,0:T(8,128)S(1)} %get-tuple-element.38.sent_ref), channel_id=1, source_target_pairs={{0,1},{1,2},{2,3},{3,0},{4,5},{5,6},{6,7},{7,4},{8,9},{9,10},{10,1... | collective-permute-start | bytes 147464 | tf_op jit(solution)/shard_map/ppermute | solution.py:436
  18.4 3.1 %copy-start = (bf16[2,20,48,128]{3,2,1,0:T(8,128)(2,1)S(1)}, bf16[2,20,48,128]{3,2,1,0:T(8,128)(2,1)}, u32[]{:S(2)}) copy-start(bf16[2,20,48,128]{3,2,1,0:T(8,128)(2,1)} %p_ref.1) | copy-start | bytes 1474564
  22.7 12.9 %collective-permute-start.6 = (f32[20,48,128]{2,1,0:T(8,128)S(1)}, f32[20,48,128]{2,1,0:T(8,128)S(1)}, u32[]{:S(2)}, u32[]{:S(2)}) collective-permute-start(f32[20,48,128]{2,1,0:T(8,128)S(1)} %restore.1), channel_id=1, source_target_pairs={{0,16},{16,0},{1,17},{17,1},{2,18},{18,2},{3,19},{19,3},{4,20},{20... | collective-permute-start | bytes 1474568 | tf_op jit(solution)/shard_map/ppermute | solution.py:436

commit v2 on v1

--- a/solution.py
+++ b/solution.py
@@ -43,7 +43,7 @@
 
 
 def dot3(a, b):
-    return dot(a[0], b[0]) + (dot(a[0], b[1]) + dot(a[1], b[0]))
+    return dot(jnp.concatenate([a[0], a[0], a[1]], 1), jnp.concatenate([b[0], b[1], b[0]], 0))
 
 
 def exact(a, b, contract=((1,), (0,))):
@@ -86,6 +86,18 @@
     return [decay * poly(d, float(steps)) for d in range(ORDER)]
 
 
+def target(place, d, blocks):
+    if blocks & (blocks - 1) == 0:
+        return place ^ d
+    return (place + d) % blocks
+
+
+def source(place, d, blocks):
+    if blocks & (blocks - 1) == 0:
+        return place ^ d
+    return (place - d + blocks) % blocks
+
+
 def section(r, states, value):
     out = []
     for s in states:
@@ -94,47 +106,27 @@
     return tuple(out)
 
 
-def project_kernel(blocks, extent, p_hbm, g_hbm, e_hbm, rx_hbm, ry_hbm, proj_ref, hat_ref, e_ref, rx_ref, ry_ref, *refs):
+def project_kernel(blocks, extent, p_hbm, g_hbm, e_hbm, rx_hbm, ry_hbm, proj_ref, z_ref, end_ref, hat_ref, e_ref, rx_ref, ry_ref, *refs):
     msg_refs = refs[: blocks - 1]
-    p_ref, g_ref, w_ref, n_ref, y_ref, sems = refs[blocks - 1 :]
+    p_ref, g_ref, mix_ref, n_ref, y_ref, sems = refs[blocks - 1 :]
     members, levels, nx, ny = p_ref.shape
     modes = e_ref.shape[1]
     rows = members * modes
     place = lax.axis_index("gx")
-    pairs = [(e_hbm, e_ref), (rx_hbm, rx_ref), (ry_hbm, ry_ref), (g_hbm, g_ref)]
-    pairs = pairs + [(p_hbm.at[m], p_ref.at[m]) for m in range(members)]
+    depth = 2 * SUB if nx % (2 * SUB) == 0 else SUB
+    pairs = [(e_hbm, e_ref), (rx_hbm, rx_ref), (ry_hbm, ry_ref), (g_hbm, g_ref), (p_hbm, p_ref)]
     copies = [pltpu.make_async_copy(a, b, sems.at[i]) for i, (a, b) in enumerate(pairs)]
     for copy in copies:
         copy.start()
     for copy in copies[:3]:
         copy.wait()
     rate = rx_ref[...]
+    pitch = n_ref.shape[0] // rows
 
     z_rows = column_of(rate, lambda i: i // SUB, modes * SUB) * (1.0 / extent)
     g_rows = gain(z_rows)
     mix = split(expanded(e_ref[...].T, modes, levels) * (g_rows * g_rows) * (g_rows * g_rows))
-    for copy in copies[3:]:
-        copy.wait()
-    for m in range(members):
-        for l in range(levels):
-            w_ref[pl.ds((m * levels + l) * nx, nx), :] = p_ref[m, l].astype(F32) * g_ref[l]
-
-    for t in range(nx // SUB):
-        wide = jnp.concatenate(
-            [
-                jnp.concatenate(
-                    [w_ref[pl.ds((m * levels + l) * nx + t * SUB, SUB), :] for l in range(levels)], 0
-                )
-                for m in range(members)
-            ],
-            1,
-        )
-        done = dot3(mix, split(wide))
-        for m in range(members):
-            for k in range(modes):
-                n_ref[pl.ds((m * modes + k) * nx + t * SUB, SUB), :] = done[
-                    k * SUB : (k + 1) * SUB, m * ny : (m + 1) * ny
-                ]
+    mix_ref[...] = jnp.concatenate([mix[0], mix[0], mix[1]], 1)
 
     z = column_of(rate, lambda i: i % modes, rows) * (1.0 / extent)
     g = gain(z)
@@ -142,21 +134,6 @@
     r = jnp.broadcast_to(jnp.exp(-z), full)
     pass_gain = jnp.broadcast_to((g * g) * (g * g), full)
     zeros = (jnp.zeros(full, F32),) * ORDER
-
-    def onward(x, states):
-        at = pl.ds(pl.multiple_of(x * rows, SUB), rows)
-        value = n_ref[pl.ds(x, rows, stride=nx), :]
-        proj_ref[at, :] = value
-        states = section(r, states, value)
-        y_ref[at, :] = states[-1] * pass_gain
-        return states
-
-    def backward(n, states):
-        x = nx - 1 - n
-        return section(r, states, y_ref[pl.ds(pl.multiple_of(x * rows, SUB), rows), :])
-
-    ends = lax.fori_loop(0, nx, onward, zeros, unroll=8)
-    starts = lax.fori_loop(0, nx, backward, zeros, unroll=8)
 
     ahead = (blocks - 1 - place) * nx
     span = (blocks - 1) * nx
@@ -177,20 +154,68 @@
             packed = jnp.where(lane == a * ORDER + b, hat[a][b], packed)
     hat_ref[...] = packed
 
+    for copy in copies[3:]:
+        copy.wait()
+    for t in range(nx // depth):
+        at = pl.ds(t * depth, depth)
+        parts = [
+            [p_ref[m, l, at, :].astype(F32) * g_ref[l, at, :] for l in range(levels)]
+            for m in range(members)
+        ]
+        for h in range(depth // SUB):
+            wide = jnp.concatenate(
+                [
+                    jnp.concatenate([part[h * SUB : (h + 1) * SUB] for part in parts[m]], 0)
+                    for m in range(members)
+                ],
+                1,
+            )
+            high, low = split(wide)
+            done = dot(mix_ref[...], jnp.concatenate([high, low, high], 0))
+            for m in range(members):
+                for k in range(modes):
+                    at = pl.ds((m * modes + k) * pitch + t * depth + h * SUB, SUB)
+                    n_ref[at, :] = done[k * SUB : (k + 1) * SUB, m * ny : (m + 1) * ny]
+
+    def onward(x, states):
+        at = pl.ds(pl.multiple_of(x * rows, SUB), rows)
+        value = n_ref[pl.ds(x, rows, stride=pitch), :]
+        proj_ref[at, :] = value
+        states = section(r, states, value)
+        y_ref[at, :] = states[-1] * pass_gain
+        return states
+
+    def backward(n, states):
+        at = pl.ds(pl.multiple_of((nx - 1 - n) * rows, SUB), rows)
+        states = section(r, states, y_ref[at, :])
+        z_ref[at, :] = states[-1]
+        return states
+
+    ends = lax.fori_loop(0, nx, onward, zeros, unroll=8)
+    starts = lax.fori_loop(0, nx, backward, zeros, unroll=8)
+
     turned = [sum(hat[a][b] * ends[b] for b in range(ORDER)) for a in range(ORDER)]
     turned = shifted(power(z, nx), turned)
     leaving = [starts[a] + turned[a] for a in range(ORDER)]
+    for a in range(ORDER):
+        end_ref[pl.ds(a * rows, rows), :] = ends[a]
+    to_right, to_left = {1: ends}, {1: leaving}
+    for hops in range(2, blocks):
+        over = power(z, (hops - 1) * nx)
+        to_right[hops] = shifted(over, ends)
+        to_left[hops] = shifted(over, leaving)
     for d in range(1, blocks):
-        to_right = ends if d == 1 else shifted(power(z, (d - 1) * nx), ends)
-        hops = blocks - d
-        to_left = leaving if hops == 1 else shifted(power(z, (hops - 1) * nx), leaving)
+        to = target(place, d, blocks)
+        reach = sorted({abs(target(i, d, blocks) - i) for i in range(blocks)})
         for a in range(ORDER):
-            msg_refs[d - 1][pl.ds(a * rows, rows), :] = jnp.where(
-                place + d < blocks, to_right[a], to_left[a]
-            )
-
-
-def table_kernel(blocks, extent, extent_x, e_ref, rx_ref, ry_ref, send_ref, high_ref, low_ref, fix_ref, lift_ref, own_ref, rise_ref, fall_ref):
+            value = to_right[reach[0]][a]
+            for hops in reach:
+                value = jnp.where(to - place == hops, to_right[hops][a], value)
+                value = jnp.where(place - to == hops, to_left[hops][a], value)
+            msg_refs[d - 1][pl.ds(a * rows, rows), :] = value
+
+
+def table_kernel(blocks, extent, extent_x, e_ref, rx_ref, ry_ref, send_ref, high_ref, low_ref, fix_ref, lift_ref, own_ref):
     modes = e_ref.shape[1]
     ny = high_ref.shape[1]
     place = lax.axis_index("gy")
@@ -258,17 +283,33 @@
     own_ref[...] = hat * pass_gain
 
     gap = iota((ny, ny), 1) - iota((ny, ny), 0)
-    rise = jnp.maximum(gap, 0).astype(F32)
-    fall = jnp.maximum(-gap, 0).astype(F32)
-    rise_ref[...] = jnp.where(gap >= 0, poly(ORDER - 1, rise + 1.0), 0.0)
-    fall_ref[...] = jnp.where(gap <= 0, poly(ORDER - 1, fall + 1.0), 0.0)
+    z_mode = ry_ref[...] * (1.0 / extent)
+    z_mode = jnp.sum(
+        jnp.where(
+            iota((modes, modes), 0) == iota((modes, modes), 1), jnp.broadcast_to(z_mode, (modes, modes)), 0.0
+        ),
+        axis=1,
+        keepdims=True,
+    )
+    lag = iota((modes, ny), 1)
+    back = jnp.where(lag == 0, 0, ny - lag).astype(F32)
+    lag = lag.astype(F32)
+    ahead_row = split(jnp.exp(-z_mode * lag) * poly(ORDER - 1, lag + 1.0))
+    back_row = split(jnp.exp(-z_mode * back) * poly(ORDER - 1, back + 1.0))
+    ahead_row = [part.astype(F32) for part in ahead_row]
+    back_row = [part.astype(F32) for part in back_row]
+
+    def band(row, inside):
+        wide = jnp.broadcast_to(row, (ny, ny))
+        wide = pltpu.roll(wide, 0, 1, stride=1, stride_axis=0)
+        return jnp.where(inside, wide, 0.0).astype(BF16)
+
     group = iota((ny, LANES), 1) // ORDER
     edge = split(sbt)
     seen = jnp.zeros((ny, LANES), F32)
     for k in range(modes):
-        rate = -z[:, k * ORDER : k * ORDER + 1]
-        up = split(jnp.exp(rise * rate) * rise_ref[...])
-        down = split(jnp.exp(fall * rate) * fall_ref[...])
+        up = [band(part[k : k + 1], gap >= 0) for part in ahead_row]
+        down = [band(part[k : k + 1], gap <= 0) for part in back_row]
         both = dot3(up, [jnp.concatenate([down[i], edge[i]], 1) for i in range(2)])
         high_ref[k], low_ref[k] = split(both[:, :ny])
         seen = jnp.where(group == k, both[:, ny:], seen)
@@ -288,24 +329,79 @@
     flip = same & (row_state + lane_state == ORDER - 1)
     turned = exact(jnp.where(flip, jnp.exp(-z_col), 0.0), seen, ((1,), (1,)))
     bent_on = exact(exact(moved(ny), hat), cbt)
-    fix_ref[0:LANES, :] = (turned + bent_on) * (gain_col * scale_col)
-    fix_ref[LANES : 2 * LANES, :] = cbt * scale_col
-
-
-def x_kernel(blocks, blocks_y, extent, proj_ref, hat_ref, rx_ref, send_ref, *refs):
+    fix = jnp.concatenate([(turned + bent_on) * (gain_col * scale_col), cbt * scale_col], 0)
+    high, low = split(fix)
+    fix_ref[...] = jnp.concatenate([high, low, high], 0)
+
+
+def lane_group(shape, modes):
+    return (iota(shape, len(shape) - 1) % (modes * ORDER)) // ORDER
+
+
+def by_mode(f_ref, z_ref, members, modes, nx):
+    for k in range(modes):
+        for m in range(members):
+            f_ref[pl.ds((k * members + m) * nx, nx), :] = z_ref[
+                pl.ds(m * modes + k, nx, stride=members * modes), :
+            ]
+
+
+def early_kernel(extent, z_ref, send_ref, rx_ref, pre_ref, react_ref, f_ref, y_ref, w_ref):
+    modes = rx_ref.shape[1]
+    nx = react_ref.shape[0] // (2 * ORDER)
+    rows = z_ref.shape[0] // nx
+    members = rows // modes
+    lines = members * nx
+    lanes = send_ref.shape[1]
+    by_mode(f_ref, z_ref, members, modes, nx)
+    wide = dot3(split(f_ref[...]), split(send_ref[...]))
+    group = lane_group((lines, lanes), modes)
+    total = jnp.zeros(group.shape, F32)
+    for k in range(modes):
+        total = jnp.where(group == k, wide[k * lines : (k + 1) * lines], total)
+    pre_ref[...] = total
+
+    full = (2 * ORDER, lanes)
+    spread = (lane_group((modes, lanes), modes) == iota((modes, lanes), 0)).astype(F32)
+    z = exact(rx_ref[...], spread) * (1.0 / extent)
+    g = gain(z)
+    r = jnp.broadcast_to(jnp.exp(-z), full)
+    pass_gain = jnp.broadcast_to((g * g) * (g * g), full)
+    unit = iota(full, 0)
+    zeros = jnp.zeros(full, F32)
+
+    def onward(x, states):
+        states = section(r, states, zeros)
+        y_ref[pl.ds(pl.multiple_of(x * SUB, SUB), SUB), :] = states[-1] * pass_gain
+        return states
+
+    def backward(n, states):
+        at = pl.ds(pl.multiple_of((nx - 1 - n) * SUB, SUB), SUB)
+        states = section(r, states, y_ref[at, :])
+        for t in range(lanes // LANES):
+            w_ref[t, at, :] = states[-1][:, t * LANES : (t + 1) * LANES]
+        return states
+
+    first = tuple((unit == a).astype(F32) for a in range(ORDER))
+    lax.fori_loop(0, nx, onward, first, unroll=8)
+    first = tuple((unit == ORDER + a).astype(F32) for a in range(ORDER))
+    lax.fori_loop(0, nx, backward, first, unroll=8)
+    for a in range(2 * ORDER):
+        for t in range(lanes // LANES):
+            react_ref[pl.ds(a * nx, nx), t * LANES : (t + 1) * LANES] = w_ref[t, pl.ds(a, nx, stride=SUB), :]
+
+
+def x_kernel(blocks, blocks_y, extent, end_ref, hat_ref, rx_ref, send_ref, pre_ref, react_ref, *refs):
     got = refs[: blocks - 1]
-    f_ref, msg_refs, y_ref, z_ref = refs[blocks - 1], refs[blocks:-2], refs[-2], refs[-1]
+    enter_ref, msg_refs = refs[blocks - 1], refs[blocks:]
     rows = hat_ref.shape[0]
     modes = rx_ref.shape[1]
     members = rows // modes
-    ny = proj_ref.shape[1]
-    nx = proj_ref.shape[0] // rows
+    ny = end_ref.shape[1]
+    nx = pre_ref.shape[0] // members
     place = lax.axis_index("gx")
     full = (rows, ny)
     z = column_of(rx_ref[...], lambda i: i % modes, rows) * (1.0 / extent)
-    g = gain(z)
-    r = jnp.broadcast_to(jnp.exp(-z), full)
-    pass_gain = jnp.broadcast_to((g * g) * (g * g), full)
 
     left, right = [], []
     for a in range(ORDER):
@@ -313,10 +409,50 @@
         b = jnp.zeros(full, F32)
         for d in range(1, blocks):
             value = got[d - 1][pl.ds(a * rows, rows), :]
-            e = e + jnp.where(place >= d, value, 0.0)
-            b = b + jnp.where(place >= d, 0.0, value)
+            behind = source(place, d, blocks) < place
+            e = e + jnp.where(behind, value, 0.0)
+            b = b + jnp.where(behind, 0.0, value)
         left.append(e)
         right.append(b)
+    ends = shifted(power(z, nx), left)
+    ends = [ends[a] + end_ref[pl.ds(a * rows, rows), :] for a in range(ORDER)]
+    hat = hat_ref[...]
+    for a in range(ORDER):
+        for b in range(ORDER):
+            at = a * ORDER + b
+            right[a] = right[a] + hat[:, at : at + 1] * ends[b]
+    enter = jnp.concatenate(left + right, 0)
+    enter_ref[...] = enter
+
+    wide = dot3(split(enter), split(send_ref[...]))
+    lanes = wide.shape[1]
+    row = iota((rows, lanes), 0)
+    mine = row % modes == lane_group((rows, lanes), modes)
+    states = modes * ORDER
+    for m in range(members):
+        here = mine & (row // modes == m)
+        total = pre_ref[pl.ds(m * nx, nx), :]
+        for a in range(2 * ORDER):
+            value = jnp.where(here, wide[a * rows : (a + 1) * rows], 0.0)
+            value = jnp.sum(value, axis=0, keepdims=True)
+            total = total + react_ref[pl.ds(a * nx, nx), :] * value
+        for d in range(blocks_y - 1):
+            moved = pltpu.roll(total, lanes - d * states, 1) if d else total
+            msg_refs[d][pl.ds(m * nx, nx), :] = moved[:, :LANES]
+
+
+def local_kernel(extent, extent_x, proj_ref, enter_ref, high_ref, low_ref, e_ref, rx_ref, ry_ref, sent_ref, own_ref, out_ref, right_ref, y_ref, z_ref, f_ref):
+    levels, modes = e_ref.shape
+    members = out_ref.shape[0] // levels
+    rows = members * modes
+    nx = out_ref.shape[1]
+    ny = proj_ref.shape[1]
+    lines = members * nx
+    full = (rows, ny)
+    z = column_of(rx_ref[...], lambda i: i % modes, rows) * (1.0 / extent_x)
+    g = gain(z)
+    r = jnp.broadcast_to(jnp.exp(-z), full)
+    pass_gain = jnp.broadcast_to((g * g) * (g * g), full)
 
     def onward(x, states):
         at = pl.ds(pl.multiple_of(x * rows, SUB), rows)
@@ -325,45 +461,21 @@
         return states
 
     def backward(n, states):
-        x = nx - 1 - n
-        at = pl.ds(pl.multiple_of(x * rows, SUB), rows)
+        at = pl.ds(pl.multiple_of((nx - 1 - n) * rows, SUB), rows)
         states = section(r, states, y_ref[at, :])
         z_ref[at, :] = states[-1]
         return states
 
-    ends = lax.fori_loop(0, nx, onward, tuple(left), unroll=8)
-    hat = hat_ref[...]
-    for a in range(ORDER):
-        for b in range(ORDER):
-            at = a * ORDER + b
-            right[a] = right[a] + hat[:, at : at + 1] * ends[b]
-    lax.fori_loop(0, nx, backward, tuple(right), unroll=8)
-
+    left = tuple(enter_ref[pl.ds(a * rows, rows), :] for a in range(ORDER))
+    lax.fori_loop(0, nx, onward, left, unroll=8)
+    right = tuple(enter_ref[pl.ds((ORDER + a) * rows, rows), :] for a in range(ORDER))
+    lax.fori_loop(0, nx, backward, right, unroll=8)
+
+    right_ref[...] = exact(sent_ref[...], own_ref[...])
+    by_mode(f_ref, z_ref, members, modes, nx)
     for k in range(modes):
-        for m in range(members):
-            f_ref[pl.ds((k * members + m) * nx, nx), :] = z_ref[pl.ds(m * modes + k, nx, stride=rows), :]
-    lines = members * nx
-    wide = dot3(split(f_ref[...]), split(send_ref[...]))
-    states = modes * ORDER
-    group = (iota((lines, wide.shape[1]), 1) % states) // ORDER
-    total = jnp.zeros(group.shape, F32)
-    for k in range(modes):
-        total = jnp.where(group == k, wide[k * lines : (k + 1) * lines], total)
-    for d in range(blocks_y - 1):
-        moved = pltpu.roll(total, total.shape[1] - d * states, 1) if d else total
-        msg_refs[d][...] = moved[:, :LANES]
-
-
-def local_kernel(extent, extent_x, z_ref, high_ref, low_ref, e_ref, rx_ref, ry_ref, out_ref, f_ref):
-    levels, modes = e_ref.shape
-    members = out_ref.shape[0] // levels
-    nx = out_ref.shape[1]
-    ny = z_ref.shape[1]
-    lines = members * nx
-    for k in range(modes):
-        high, low = split(z_ref[pl.ds(k * lines, lines), :])
-        wide = dot(high, jnp.concatenate([high_ref[k], low_ref[k]], 1))
-        f_ref[pl.ds(k * lines, lines), :] = wide[:, :ny] + (wide[:, ny:] + dot(low, high_ref[k]))
+        at = pl.ds(k * lines, lines)
+        f_ref[at, :] = dot3(split(f_ref[at, :]), (high_ref[k], low_ref[k]))
     g = gain(ry_ref[...] * (1.0 / extent))
     gx = gain(rx_ref[...] * (1.0 / extent_x))
     pass_gain = (g * g) * (g * g)
@@ -387,27 +499,28 @@
                 ]
 
 
-def final_kernel(blocks, total_members, p_ref, base_ref, fix_ref, lift_ref, own_ref, sent_ref, *refs):
+def final_kernel(blocks, total_members, first, p_ref, base_ref, right_ref, fix_ref, lift_ref, *refs):
     got, out_ref = refs[:-1], refs[-1]
     members, levels, nx, ny = p_ref.shape
     place = lax.axis_index("gy")
     left = jnp.zeros(got[0].shape, F32)
-    right = exact(sent_ref[...], own_ref[...])
+    right = right_ref[...]
     for d in range(1, blocks):
         value = got[d - 1][...]
         left = left + jnp.where(place >= d, value, 0.0)
         right = right + jnp.where(place >= d, 0.0, value)
     enter = jnp.concatenate([left, right], 1)
-    fix = split(fix_ref[...])
+    fix = fix_ref[...]
     share = 1.0 / (total_members - 1)
-    for l in range(levels):
-        add = dot3(split(enter * lift_ref[pl.ds(l, 1), :]), fix)
+    for l in range(first, first + out_ref.shape[0]):
+        high, low = split(enter * lift_ref[pl.ds(l, 1), :])
+        add = dot(jnp.concatenate([high, high, low], 1), fix)
         out = jnp.zeros((nx, ny), F32)
         for m in range(members):
             out = out + p_ref[m, l].astype(F32) * (
                 base_ref[m * levels + l] + add[m * nx : (m + 1) * nx]
             )
-        out_ref[l] = out * share
+        out_ref[l - first] = out * share
 
 
 def call(kernel, out, ins, scratch=(), far=False, flops=0, name=None):
@@ -431,9 +544,12 @@
     return jax.ShapeDtypeStruct(dims, F32)
 
 
-def turn(value, axis, distance):
+def exchange(values, axis, order, to):
     n = lax.axis_size(axis)
-    return lax.ppermute(value, axis, [(i, (i + distance) % n) for i in range(n)])
+    got = {
+        d: lax.ppermute(values[d - 1], axis, [(i, to(i, d, n)) for i in range(n)]) for d in order
+    }
+    return [got[d] for d in range(1, n)]
 
 
 def body(perturb, gradient, vertical_eigenmodes, rate_x, rate_y):
@@ -443,10 +559,13 @@
     blocks_x, blocks_y = lax.axis_size("gx"), lax.axis_size("gy")
     extent_x, extent_y = nx * blocks_x, ny * blocks_y
 
-    proj, hat, eigen, row_x, row_y, *messages = call(
+    field = shape(rows * nx, ny)
+    pitch = (nx // SUB | 1) * SUB
+    proj, alone, ends, hat, eigen, row_x, row_y, *messages = call(
         functools.partial(project_kernel, blocks_x, extent_x),
         tuple(
-            [shape(rows * nx, ny), shape(rows, LANES), shape(levels, modes), shape(1, modes), shape(1, modes)]
+            [field, field, shape(ORDER * rows, ny), shape(rows, LANES)]
+            + [shape(levels, modes), shape(1, modes), shape(1, modes)]
             + [shape(ORDER * rows, ny)] * (blocks_x - 1)
         ),
         tuple(
@@ -456,53 +575,76 @@
         scratch=(
             VMEM(perturb.shape, perturb.dtype),
             VMEM(gradient.shape, F32),
-            VMEM((members * levels * nx, ny), F32),
+            VMEM((modes * SUB, 3 * levels * SUB), BF16),
+            VMEM((rows * pitch, ny), F32),
             VMEM((rows * nx, ny), F32),
-            VMEM((rows * nx, ny), F32),
-            pltpu.SemaphoreType.DMA((4 + members,)),
+            pltpu.SemaphoreType.DMA((5,)),
         ),
         far=True,
         flops=1 << 28,
         name="project",
     )
-    got = [turn(messages[d - 1], "gx", d) for d in range(1, blocks_x)]
+    got = exchange(messages, "gx", [1] + list(range(blocks_x - 1, 1, -1)), target)
     packed = -(-(blocks_y - 1) * modes * ORDER // LANES) * LANES
     half = jax.ShapeDtypeStruct((modes, ny, ny), BF16)
     send, high, low, fix, lift, own = call(
         functools.partial(table_kernel, blocks_y, extent_y, extent_x),
-        (shape(ny, packed), half, half, shape(2 * LANES, ny), shape(levels, 2 * LANES), shape(LANES, LANES)),
+        (
+            shape(ny, packed),
+            half,
+            half,
+            jax.ShapeDtypeStruct((6 * LANES, ny), BF16),
+            shape(levels, 2 * LANES),
+            shape(LANES, LANES),
+        ),
         (eigen, row_x, row_y),
-        scratch=(VMEM((ny, ny), F32), VMEM((ny, ny), F32)),
         flops=1 << 30,
         name="tables",
     )
-    filtered, *sent = call(
+    before, react = call(
+        functools.partial(early_kernel, extent_x),
+        (shape(members * nx, packed), shape(2 * ORDER * nx, packed)),
+        (alone, send, row_x),
+        scratch=(
+            VMEM((rows * nx, ny), F32),
+            VMEM((SUB * nx, packed), F32),
+            VMEM((packed // LANES, SUB * nx, LANES), F32),
+        ),
+        flops=1 << 29,
+        name="early",
+    )
+    enter, *sent = call(
         functools.partial(x_kernel, blocks_x, blocks_y, extent_x),
-        tuple([shape(rows * nx, ny)] + [shape(members * nx, LANES)] * (blocks_y - 1)),
-        (proj, hat, row_x, send, *got),
-        scratch=(VMEM((rows * nx, ny), F32), VMEM((rows * nx, ny), F32)),
-        flops=1 << 28,
+        tuple([shape(2 * ORDER * rows, ny)] + [shape(members * nx, LANES)] * (blocks_y - 1)),
+        (ends, hat, row_x, send, before, react, *got),
+        flops=1 << 27,
         name="along_x",
     )
-    got = [turn(sent[d - 1], "gy", d) for d in range(1, blocks_y)]
-    base = call(
+    got = exchange(sent, "gy", list(range(blocks_y - 1, 0, -1)), lambda i, d, n: (i + d) % n)
+    base, right = call(
         functools.partial(local_kernel, extent_y, extent_x),
-        shape(members * levels, nx, ny),
-        (filtered, high, low, eigen, row_x, row_y),
-        scratch=(VMEM((rows * nx, ny), F32),),
+        (shape(members * levels, nx, ny), shape(members * nx, LANES)),
+        (proj, enter, high, low, eigen, row_x, row_y, sent[0], own),
+        scratch=(VMEM((rows * nx, ny), F32),) * 3,
         flops=1 << 29,
         name="along_y",
     )
-    partial = call(
-        functools.partial(final_kernel, blocks_y, members * lax.axis_size("member")),
-        shape(levels, nx, ny),
-        (perturb, base, fix, lift, own, sent[0], *got),
-        flops=1 << 28,
-        name="restore",
-    )
-    if lax.axis_size("member") == 2:
-        return partial + turn(partial, "member", 1)
-    return lax.psum(partial, "member")
+    pieces = 4 if levels % 4 == 0 else 1
+    size = levels // pieces
+    parts = [
+        call(
+            functools.partial(final_kernel, blocks_y, members * lax.axis_size("member"), i * size),
+            shape(size, nx, ny),
+            (perturb, base, right, fix, lift, *got),
+            flops=1 << 27,
+            name="restore",
+        )
+        for i in range(pieces)
+    ]
+    if lax.axis_size("member") > 2:
+        return lax.psum(jnp.concatenate(parts, 0), "member")
+    others = [lax.ppermute(part, "member", [(0, 1), (1, 0)]) for part in parts]
+    return jnp.concatenate([a + b for a, b in zip(parts, others)], 0)
 
 
 def solution(mesh):

time: 36.7 us -> 35.2 us (0.959)
  waiting for transfers between devices: 14.2 us -> 11 us
  starting transfers between devices: 10.7 us -> 12.1 us
    ppermute x7 -> x10, waiting for transfers between devices: 14.2 us -> 11 us  [the longest x4 7.39 us: body(): others = [lax.ppermute(part, 'member', [(0, 1), (1, 0)]) for part in parts]]
    ppermute x7 -> x10, starting transfers between devices: 10.7 us -> 12.1 us  [the longest x6 7.8 us: exchange(): lax.ppermute(values[d - 1], axis, [(i, to(i, d, n)) for i in range(n)])]
    concatenate x0 -> x1, other arithmetic: none -> 0.83 us  [body(): return jnp.concatenate([a + b for a, b in zip(parts, others)], 0)]
    add x1 -> x4, other arithmetic: 0.84 us -> 0.07 us  [body(): return jnp.concatenate([a + b for a, b in zip(parts, others)], 0)]
    pallas_call x5 -> x9, Pallas kernels: 10.6 us -> 10.8 us  [call(): pl.pallas_call(kernel, out_shape=out, in_specs=[spec(i) for i in range(le...]
  transfers between devices with their start and end apart: 7 -> 10, of which waited for: 6 -> 6; matrix products, arithmetic and copies ran while one was open for 0% -> 0% of each run, Pallas kernels for 12% -> 20%
where the time goes in v2:
time: 35.2 us; the launch traced here: 35 us
  starting transfers between devices  12.1 us (34%)
  waiting for transfers between devices  11 us (31%)
  Pallas kernels  10.8 us (31%)
  other arithmetic  0.89 us (3%)
    pallas_call x9, Pallas kernels, call(): pl.pallas_call(kernel, out_shape=out, in_specs=[spec(i) for i in range(le...  10.8 us
    ppermute x6, starting transfers between devices, exchange(): lax.ppermute(values[d - 1], axis, [(i, to(i, d, n)) for i in range(n)])  7.8 us
    ppermute x4, waiting for transfers between devices, body(): others = [lax.ppermute(part, 'member', [(0, 1), (1, 0)]) for part in parts]  7.39 us
    ppermute x4, starting transfers between devices, body(): others = [lax.ppermute(part, 'member', [(0, 1), (1, 0)]) for part in parts]  4.32 us
    ppermute x6, waiting for transfers between devices, exchange(): lax.ppermute(values[d - 1], axis, [(i, to(i, d, n)) for i in range(n)])  3.63 us
    concatenate x1, other arithmetic, body(): return jnp.concatenate([a + b for a, b in zip(parts, others)], 0)  0.83 us
  transfers between devices with their start and end apart: 10, of which 6 were waited for; matrix products, arithmetic and copies ran while one was open for 0% of the time, Pallas kernels for 20%

profile of v2, /device:TPU:0, one launch (start us, length us, event | category | flops | bytes accessed | tf_op | source)
XLA Modules:
  0.0 35.0 jit_solution(15219474233568161568)
XLA Ops:
  0.0 2.8 %project.1 = (f32[1920,128]{1,0:T(8,128)S(1)}, f32[1920,128]{1,0:T(8,128)S(1)}, f32[160,128]{1,0:T(8,128)S(1)}, f32[40,128]{1,0:T(8,128)S(1)}, f32[20,20]{1,0:T(...) custom-call(bf16[2,20,48,128]{3,2,1,0:T(8,128)(2,1)} %p_ref.7, ...), custom_call_target="tpu_custom_call" | custom-call | flops 268435456 | bytes 3300800 | tf_op jit(solution)/shard_map/project/pallas_call | solution.py:531
  2.8 3.1 %collective-permute-start = (f32[160,128]{1,0:T(8,128)S(1)}, f32[160,128]{1,0:T(8,128)S(1)}, u32[]{:S(2)}, u32[]{:S(2)}) collective-permute-start(f32[160,128]{1,0:T(8,128)S(1)} %get-tuple-element.39), channel_id=1, source_target_pairs={{0,4},{4,0},{8,12},{12,8},{1,5},{5,1},{9,13},{13,9},{2,6},{6,2},{1... | collective-permute-start | bytes 245768 | tf_op jit(solution)/shard_map/ppermute | solution.py:550
  5.9 2.6 %collective-permute-start.1 = (f32[160,128]{1,0:T(8,128)S(1)}, f32[160,128]{1,0:T(8,128)S(1)}, u32[]{:S(2)}, u32[]{:S(2)}) collective-permute-start(f32[160,128]{1,0:T(8,128)S(1)} %get-tuple-element.40), channel_id=1, source_target_pairs={{0,8},{4,12},{8,0},{12,4},{1,9},{5,13},{9,1},{13,5},{2,10},{6,14},... | collective-permute-start | bytes 245768 | tf_op jit(solution)/shard_map/ppermute | solution.py:550
  8.5 0.0 collective-permute-start.2
  8.5 2.6 %tables.1 = (f32[128,256]{1,0:T(8,128)S(1)}, bf16[20,128,128]{2,1,0:T(8,128)(2,1)S(1)}, bf16[20,128,128]{2,1,0:T(8,128)(2,1)S(1)}, bf16[768,128]{1,0:T(8,128)(2,...) custom-call(f32[20,20]{1,0:T(8,128)S(1)} %get-tuple-element.33.e_ref, f32[1,20]{1,0:T(1,128)S(1)} %get-tuple-element.32.rx_ref, ...), custom_call_target="tpu_custom_call" | custom-call | flops 1073741824 | bytes 1726176 | tf_op jit(solution)/shard_map/tables/pallas_call | solution.py:531
  11.1 1.1 %early.1 = (f32[96,256]{1,0:T(8,128)S(1)}, f32[384,256]{1,0:T(8,128)S(1)}) custom-call(f32[1920,128]{1,0:T(8,128)S(1)} %get-tuple-element.36.z_ref, f32[128,256]{1,0:T(8,128)S(1)} %get-tuple-element.35.send_ref, f32[1,20]{1,0:T(1,128)S(1)} %get-tuple-element.32.rx_ref), custom_call_target="tpu_custom_call" | custom-call | flops 536870912 | bytes 1605712 | tf_op jit(solution)/shard_map/early/pallas_call | solution.py:531
  12.2 0.0 collective-permute-done.refs_0_
  12.2 2.9 %collective-permute-done.1.refs_1_ = f32[160,128]{1,0:T(8,128)S(1)} collective-permute-done((f32[160,128]{1,0:T(8,128)S(1)}, f32[160,128]{1,0:T(8,128)S(1)}, u32[]{:S(2)}, u32[]{:S(2)}) %collective-permute-start.1) | collective-permute-done | bytes 81952 | tf_op jit(solution)/shard_map/ppermute | solution.py:550
  15.1 0.0 collective-permute-done.2.refs_2_
  15.1 0.5 %along_x.1 = (f32[320,128]{1,0:T(8,128)S(1)}, f32[96,128]{1,0:T(8,128)S(1)}, f32[96,128]{1,0:T(8,128)S(1)}, f32[96,128]{1,0:T(8,128)S(1)}) custom-call(f32[160,128]{1,0:T(8,128)S(1)} %get-tuple-element.30.end_ref, f32[40,128]{1,0:T(8,128)S(1)} %get-tuple-element.31.hat_ref, f32[1,20]{1,0:T(1,128)S(1)} %get-tuple-element.32.rx_ref, ...), custom_call_target="tpu_custom_call" | custom-call | flops 134217728 | bytes 1282128 | tf_op jit(solution)/shard_map/along_x/pallas_call | solution.py:531
  15.7 1.6 %collective-permute-start.4 = (f32[96,128]{1,0:T(8,128)S(1)}, f32[96,128]{1,0:T(8,128)S(1)}, u32[]{:S(2)}, u32[]{:S(2)}) collective-permute-start(f32[96,128]{1,0:T(8,128)S(1)} %get-tuple-element.51), channel_id=1, source_target_pairs={{0,2},{1,3},{2,0},{3,1},{4,6},{5,7},{6,4},{7,5},{8,10},{9,11},{10,... | collective-permute-start | bytes 147464 | tf_op jit(solution)/shard_map/ppermute | solution.py:550
  17.2 0.0 collective-permute-start.5
  17.2 0.5 %collective-permute-start.3 = (f32[96,128]{1,0:T(8,128)S(1)}, f32[96,128]{1,0:T(8,128)S(1)}, u32[]{:S(2)}, u32[]{:S(2)}) collective-permute-start(f32[96,128]{1,0:T(8,128)S(1)} %get-tuple-element.45.sent_ref), channel_id=1, source_target_pairs={{0,1},{1,2},{2,3},{3,0},{4,5},{5,6},{6,7},{7,4},{8,9},{9,10},{10,1... | collective-permute-start | bytes 147464 | tf_op jit(solution)/shard_map/ppermute | solution.py:550
  17.8 0.0 copy-start
  17.8 2.4 %along_y.1 = (f32[40,48,128]{2,1,0:T(8,128)S(1)}, f32[96,128]{1,0:T(8,128)S(1)}) custom-call(f32[1920,128]{1,0:T(8,128)S(1)} %get-tuple-element.29.proj_ref, f32[320,128]{1,0:T(8,128)S(1)} %get-tuple-element.42.enter_ref, bf16[20,128,128]{2,1,0:T(8,128)(2,1)S(1)} %get-tuple-element.43.high_ref, bf16[20,128,128]{2,1,0:T(8,128)(2,1)S(1)} %get-tuple-element.44.low_ref, ...), custom_call_target="tpu_custom_call" | custom-call | flops 536870912 | bytes 3606240 | tf_op jit(solution)/shard_map/along_y/pallas_call | solution.py:531
  20.1 0.0 collective-permute-done.4.refs_1_
  20.1 0.0 collective-permute-done.5.refs_2_
  20.2 0.7 %collective-permute-done.3.refs_0_ = f32[96,128]{1,0:T(8,128)S(1)} collective-permute-done((f32[96,128]{1,0:T(8,128)S(1)}, f32[96,128]{1,0:T(8,128)S(1)}, u32[]{:S(2)}, u32[]{:S(2)}) %collective-permute-start.3) | collective-permute-done | bytes 49184 | tf_op jit(solution)/shard_map/ppermute | solution.py:550
  20.9 0.0 copy-done
  20.9 0.4 %restore.4 = f32[5,48,128]{2,1,0:T(8,128)S(1)} custom-call(bf16[2,20,48,128]{3,2,1,0:T(8,128)(2,1)S(1)} %copy-done, f32[40,48,128]{2,1,0:T(8,128)S(1)} %get-tuple-element.47.base_ref, f32[96,128]{1,0:T(8,128)S(1)} %get-tuple-element.48.right_ref, bf16[768,128]{1,0:T(8,128)(2,1)S(1)} %get-tuple-element.49.fix_ref, f32[20,256]{1,0:T(8,128)S(1)} %get-tuple-element.50.lift_ref, ...), custom_call_target="tpu_custom_call" | custom-call | flops 134217728 | bytes 2011136 | tf_op jit(solution)/shard_map/restore/pallas_call | solution.py:531
  21.2 1.6 %collective-permute-start.6 = (f32[5,48,128]{2,1,0:T(8,128)S(1)}, f32[5,48,128]{2,1,0:T(8,128)S(1)}, u32[]{:S(2)}, u32[]{:S(2)}) collective-permute-start(f32[5,48,128]{2,1,0:T(8,128)S(1)} %restore.4), channel_id=1, source_target_pairs={{0,16},{16,0},{1,17},{17,1},{2,18},{18,2},{3,19},{19,3},{4,20},{20... | collective-permute-start | bytes 368648 | tf_op jit(solution)/shard_map/ppermute | solution.py:646
  22.8 0.4 %restore.5 = f32[5,48,128]{2,1,0:T(8,128)S(1)} custom-call(bf16[2,20,48,128]{3,2,1,0:T(8,128)(2,1)S(1)} %copy-done, f32[40,48,128]{2,1,0:T(8,128)S(1)} %get-tuple-element.47.base_ref, f32[96,128]{1,0:T(8,128)S(1)} %get-tuple-element.48.right_ref, bf16[768,128]{1,0:T(8,128)(2,1)S(1)} %get-tuple-element.49.fix_ref, f32[20,256]{1,0:T(8,128)S(1)} %get-tuple-element.50.lift_ref, ...), custom_call_target="tpu_custom_call" | custom-call | flops 134217728 | bytes 2011136 | tf_op jit(solution)/shard_map/restore/pallas_call | solution.py:531
  23.2 0.6 %collective-permute-start.7 = (f32[5,48,128]{2,1,0:T(8,128)S(1)}, f32[5,48,128]{2,1,0:T(8,128)S(1)}, u32[]{:S(2)}, u32[]{:S(2)}) collective-permute-start(f32[5,48,128]{2,1,0:T(8,128)S(1)} %restore.5), channel_id=1, source_target_pairs={{0,16},{16,0},{1,17},{17,1},{2,18},{18,2},{3,19},{19,3},{4,20},{20... | collective-permute-start | bytes 368648 | tf_op jit(solution)/shard_map/ppermute | solution.py:646
  23.8 0.4 %restore.6 = f32[5,48,128]{2,1,0:T(8,128)S(1)} custom-call(bf16[2,20,48,128]{3,2,1,0:T(8,128)(2,1)S(1)} %copy-done, f32[40,48,128]{2,1,0:T(8,128)S(1)} %get-tuple-element.47.base_ref, f32[96,128]{1,0:T(8,128)S(1)} %get-tuple-element.48.right_ref, bf16[768,128]{1,0:T(8,128)(2,1)S(1)} %get-tuple-element.49.fix_ref, f32[20,256]{1,0:T(8,128)S(1)} %get-tuple-element.50.lift_ref, ...), custom_call_target="tpu_custom_call" | custom-call | flops 134217728 | bytes 2011136 | tf_op jit(solution)/shard_map/restore/pallas_call | solution.py:531
  24.1 1.6 %collective-permute-start.8 = (f32[5,48,128]{2,1,0:T(8,128)S(1)}, f32[5,48,128]{2,1,0:T(8,128)S(1)}, u32[]{:S(2)}, u32[]{:S(2)}) collective-permute-start(f32[5,48,128]{2,1,0:T(8,128)S(1)} %restore.6), channel_id=1, source_target_pairs={{0,16},{16,0},{1,17},{17,1},{2,18},{18,2},{3,19},{19,3},{4,20},{20... | collective-permute-start | bytes 368648 | tf_op jit(solution)/shard_map/ppermute | solution.py:646
  25.7 0.4 %restore.7 = f32[5,48,128]{2,1,0:T(8,128)S(1)} custom-call(bf16[2,20,48,128]{3,2,1,0:T(8,128)(2,1)S(1)} %copy-done, f32[40,48,128]{2,1,0:T(8,128)S(1)} %get-tuple-element.47.base_ref, f32[96,128]{1,0:T(8,128)S(1)} %get-tuple-element.48.right_ref, bf16[768,128]{1,0:T(8,128)(2,1)S(1)} %get-tuple-element.49.fix_ref, f32[20,256]{1,0:T(8,128)S(1)} %get-tuple-element.50.lift_ref, ...), custom_call_target="tpu_custom_call" | custom-call | flops 134217728 | bytes 2011136 | tf_op jit(solution)/shard_map/restore/pallas_call | solution.py:531
  26.1 0.6 %collective-permute-start.9 = (f32[5,48,128]{2,1,0:T(8,128)S(1)}, f32[5,48,128]{2,1,0:T(8,128)S(1)}, u32[]{:S(2)}, u32[]{:S(2)}) collective-permute-start(f32[5,48,128]{2,1,0:T(8,128)S(1)} %restore.7), channel_id=1, source_target_pairs={{0,16},{16,0},{1,17},{17,1},{2,18},{18,2},{3,19},{19,3},{4,20},{20... | collective-permute-start | bytes 368648 | tf_op jit(solution)/shard_map/ppermute | solution.py:646
  26.7 0.5 %collective-permute-done.6 = f32[5,48,128]{2,1,0:T(8,128)S(1)} collective-permute-done((f32[5,48,128]{2,1,0:T(8,128)S(1)}, f32[5,48,128]{2,1,0:T(8,128)S(1)}, u32[]{:S(2)}, u32[]{:S(2)}) %collective-permute-start.6) | collective-permute-done | bytes 122912 | tf_op jit(solution)/shard_map/ppermute | solution.py:646
  27.2 2.6 %collective-permute-done.7 = f32[5,48,128]{2,1,0:T(8,128)S(1)} collective-permute-done((f32[5,48,128]{2,1,0:T(8,128)S(1)}, f32[5,48,128]{2,1,0:T(8,128)S(1)}, u32[]{:S(2)}, u32[]{:S(2)}) %collective-permute-start.7) | collective-permute-done | bytes 122912 | tf_op jit(solution)/shard_map/ppermute | solution.py:646
  29.8 2.6 %collective-permute-done.8 = f32[5,48,128]{2,1,0:T(8,128)S(1)} collective-permute-done((f32[5,48,128]{2,1,0:T(8,128)S(1)}, f32[5,48,128]{2,1,0:T(8,128)S(1)}, u32[]{:S(2)}, u32[]{:S(2)}) %collective-permute-start.8) | collective-permute-done | bytes 122912 | tf_op jit(solution)/shard_map/ppermute | solution.py:646
  32.5 1.7 %collective-permute-done.9 = f32[5,48,128]{2,1,0:T(8,128)S(1)} collective-permute-done((f32[5,48,128]{2,1,0:T(8,128)S(1)}, f32[5,48,128]{2,1,0:T(8,128)S(1)}, u32[]{:S(2)}, u32[]{:S(2)}) %collective-permute-start.9) | collective-permute-done | bytes 122912 | tf_op jit(solution)/shard_map/ppermute | solution.py:646
  34.1 0.8 %pad_maximum_fusion = f32[20,48,128]{2,1,0:T(8,128)} fusion(f32[5,48,128]{2,1,0:T(8,128)S(1)} %add.15, f32[5,48,128]{2,1,0:T(8,128)S(1)} %add.14, f32[5,48,128]{2,1,0:T(8,128)S(1)} %add.13, f32[5,48,128]{2,1,0:T(8,128)S(1)} %add.12), kind=kLoop, calls=%fused_computation | loop fusion | flops 368640 | bytes 983040 | tf_op jit(solution)/shard_map/concatenate | solution.py:647
  (4 shorter events, 0.1 us)
Async XLA Ops:
  2.8 9.4 %collective-permute-start = (f32[160,128]{1,0:T(8,128)S(1)}, f32[160,128]{1,0:T(8,128)S(1)}, u32[]{:S(2)}, u32[]{:S(2)}) collective-permute-start(f32[160,128]{1,0:T(8,128)S(1)} %get-tuple-element.39), channel_id=1, source_target_pairs={{0,4},{4,0},{8,12},{12,8},{1,5},{5,1},{9,13},{13,9},{2,6},{6,2},{1... | collective-permute-start | bytes 245768 | tf_op jit(solution)/shard_map/ppermute | solution.py:550
  5.9 9.2 %collective-permute-start.1 = (f32[160,128]{1,0:T(8,128)S(1)}, f32[160,128]{1,0:T(8,128)S(1)}, u32[]{:S(2)}, u32[]{:S(2)}) collective-permute-start(f32[160,128]{1,0:T(8,128)S(1)} %get-tuple-element.40), channel_id=1, source_target_pairs={{0,8},{4,12},{8,0},{12,4},{1,9},{5,13},{9,1},{13,5},{2,10},{6,14},... | collective-permute-start | bytes 245768 | tf_op jit(solution)/shard_map/ppermute | solution.py:550
  8.5 6.6 %collective-permute-start.2 = (f32[160,128]{1,0:T(8,128)S(1)}, f32[160,128]{1,0:T(8,128)S(1)}, u32[]{:S(2)}, u32[]{:S(2)}) collective-permute-start(f32[160,128]{1,0:T(8,128)S(1)} %get-tuple-element.41), channel_id=1, source_target_pairs={{0,12},{4,8},{8,4},{12,0},{1,13},{5,9},{9,5},{13,1},{2,14},{6,10},... | collective-permute-start | bytes 245768 | tf_op jit(solution)/shard_map/ppermute | solution.py:550
  15.7 4.5 %collective-permute-start.4 = (f32[96,128]{1,0:T(8,128)S(1)}, f32[96,128]{1,0:T(8,128)S(1)}, u32[]{:S(2)}, u32[]{:S(2)}) collective-permute-start(f32[96,128]{1,0:T(8,128)S(1)} %get-tuple-element.51), channel_id=1, source_target_pairs={{0,2},{1,3},{2,0},{3,1},{4,6},{5,7},{6,4},{7,5},{8,10},{9,11},{10,... | collective-permute-start | bytes 147464 | tf_op jit(solution)/shard_map/ppermute | solution.py:550
  17.2 2.9 %collective-permute-start.5 = (f32[96,128]{1,0:T(8,128)S(1)}, f32[96,128]{1,0:T(8,128)S(1)}, u32[]{:S(2)}, u32[]{:S(2)}) collective-permute-start(f32[96,128]{1,0:T(8,128)S(1)} %get-tuple-element.52), channel_id=1, source_target_pairs={{0,3},{1,0},{2,1},{3,2},{4,7},{5,4},{6,5},{7,6},{8,11},{9,8},{10,9... | collective-permute-start | bytes 147464 | tf_op jit(solution)/shard_map/ppermute | solution.py:550
  17.2 3.6 %collective-permute-start.3 = (f32[96,128]{1,0:T(8,128)S(1)}, f32[96,128]{1,0:T(8,128)S(1)}, u32[]{:S(2)}, u32[]{:S(2)}) collective-permute-start(f32[96,128]{1,0:T(8,128)S(1)} %get-tuple-element.45.sent_ref), channel_id=1, source_target_pairs={{0,1},{1,2},{2,3},{3,0},{4,5},{5,6},{6,7},{7,4},{8,9},{9,10},{10,1... | collective-permute-start | bytes 147464 | tf_op jit(solution)/shard_map/ppermute | solution.py:550
  17.8 3.1 %copy-start = (bf16[2,20,48,128]{3,2,1,0:T(8,128)(2,1)S(1)}, bf16[2,20,48,128]{3,2,1,0:T(8,128)(2,1)}, u32[]{:S(2)}) copy-start(bf16[2,20,48,128]{3,2,1,0:T(8,128)(2,1)} %p_ref.7) | copy-start | bytes 1474564
  21.2 5.9 %collective-permute-start.6 = (f32[5,48,128]{2,1,0:T(8,128)S(1)}, f32[5,48,128]{2,1,0:T(8,128)S(1)}, u32[]{:S(2)}, u32[]{:S(2)}) collective-permute-start(f32[5,48,128]{2,1,0:T(8,128)S(1)} %restore.4), channel_id=1, source_target_pairs={{0,16},{16,0},{1,17},{17,1},{2,18},{18,2},{3,19},{19,3},{4,20},{20... | collective-permute-start | bytes 368648 | tf_op jit(solution)/shard_map/ppermute | solution.py:646
  23.2 6.6 %collective-permute-start.7 = (f32[5,48,128]{2,1,0:T(8,128)S(1)}, f32[5,48,128]{2,1,0:T(8,128)S(1)}, u32[]{:S(2)}, u32[]{:S(2)}) collective-permute-start(f32[5,48,128]{2,1,0:T(8,128)S(1)} %restore.5), channel_id=1, source_target_pairs={{0,16},{16,0},{1,17},{17,1},{2,18},{18,2},{3,19},{19,3},{4,20},{20... | collective-permute-start | bytes 368648 | tf_op jit(solution)/shard_map/ppermute | solution.py:646
  24.1 8.3 %collective-permute-start.8 = (f32[5,48,128]{2,1,0:T(8,128)S(1)}, f32[5,48,128]{2,1,0:T(8,128)S(1)}, u32[]{:S(2)}, u32[]{:S(2)}) collective-permute-start(f32[5,48,128]{2,1,0:T(8,128)S(1)} %restore.6), channel_id=1, source_target_pairs={{0,16},{16,0},{1,17},{17,1},{2,18},{18,2},{3,19},{19,3},{4,20},{20... | collective-permute-start | bytes 368648 | tf_op jit(solution)/shard_map/ppermute | solution.py:646
  26.1 8.0 %collective-permute-start.9 = (f32[5,48,128]{2,1,0:T(8,128)S(1)}, f32[5,48,128]{2,1,0:T(8,128)S(1)}, u32[]{:S(2)}, u32[]{:S(2)}) collective-permute-start(f32[5,48,128]{2,1,0:T(8,128)S(1)} %restore.7), channel_id=1, source_target_pairs={{0,16},{16,0},{1,17},{17,1},{2,18},{18,2},{3,19},{19,3},{4,20},{20... | collective-permute-start | bytes 368648 | tf_op jit(solution)/shard_map/ppermute | solution.py:646

commit v3 on v2

--- a/solution.py
+++ b/solution.py
@@ -523,20 +523,19 @@
         out_ref[l - first] = out * share
 
 
-def call(kernel, out, ins, scratch=(), far=False, flops=0, name=None):
-    spec = lambda i: pl.BlockSpec(memory_space=pltpu.HBM if far else VMEM)
+def call(kernel, out, ins, scratch=(), far=False, flops=0):
+    spec = lambda: pl.BlockSpec(memory_space=pltpu.HBM if far else VMEM)
     nbytes = sum(a.size * a.dtype.itemsize for a in ins) + sum(
         a.size * a.dtype.itemsize for a in jax.tree.leaves(out)
     )
     return pl.pallas_call(
         kernel,
         out_shape=out,
-        in_specs=[spec(i) for i in range(len(ins))],
+        in_specs=[spec() for _ in range(len(ins))],
         out_specs=jax.tree.map(lambda _: pl.BlockSpec(memory_space=VMEM), out),
         scratch_shapes=list(scratch),
         cost_estimate=pl.CostEstimate(flops=flops, bytes_accessed=nbytes, transcendentals=0),
         compiler_params=pltpu.CompilerParams(vmem_limit_bytes=GRANT),
-        name=name,
     )(*ins)
 
 
@@ -544,12 +543,12 @@
     return jax.ShapeDtypeStruct(dims, F32)
 
 
-def exchange(values, axis, order, to):
+def exchange(values, axis, to):
     n = lax.axis_size(axis)
-    got = {
-        d: lax.ppermute(values[d - 1], axis, [(i, to(i, d, n)) for i in range(n)]) for d in order
-    }
-    return [got[d] for d in range(1, n)]
+    got = []
+    for d in range(1, n):
+        got.append(lax.ppermute(values[d - 1], axis, [(i, to(i, d, n)) for i in range(n)]))
+    return got
 
 
 def body(perturb, gradient, vertical_eigenmodes, rate_x, rate_y):
@@ -582,9 +581,8 @@
         ),
         far=True,
         flops=1 << 28,
-        name="project",
-    )
-    got = exchange(messages, "gx", [1] + list(range(blocks_x - 1, 1, -1)), target)
+    )
+    got = exchange(messages, "gx", target)
     packed = -(-(blocks_y - 1) * modes * ORDER // LANES) * LANES
     half = jax.ShapeDtypeStruct((modes, ny, ny), BF16)
     send, high, low, fix, lift, own = call(
@@ -599,7 +597,6 @@
         ),
         (eigen, row_x, row_y),
         flops=1 << 30,
-        name="tables",
     )
     before, react = call(
         functools.partial(early_kernel, extent_x),
@@ -611,23 +608,20 @@
             VMEM((packed // LANES, SUB * nx, LANES), F32),
         ),
         flops=1 << 29,
-        name="early",
     )
     enter, *sent = call(
         functools.partial(x_kernel, blocks_x, blocks_y, extent_x),
         tuple([shape(2 * ORDER * rows, ny)] + [shape(members * nx, LANES)] * (blocks_y - 1)),
         (ends, hat, row_x, send, before, react, *got),
         flops=1 << 27,
-        name="along_x",
-    )
-    got = exchange(sent, "gy", list(range(blocks_y - 1, 0, -1)), lambda i, d, n: (i + d) % n)
+    )
+    got = exchange(sent, "gy", lambda i, d, n: (i + d) % n)
     base, right = call(
         functools.partial(local_kernel, extent_y, extent_x),
         (shape(members * levels, nx, ny), shape(members * nx, LANES)),
         (proj, enter, high, low, eigen, row_x, row_y, sent[0], own),
         scratch=(VMEM((rows * nx, ny), F32),) * 3,
         flops=1 << 29,
-        name="along_y",
     )
     pieces = 4 if levels % 4 == 0 else 1
     size = levels // pieces
@@ -637,7 +631,6 @@
             shape(size, nx, ny),
             (perturb, base, right, fix, lift, *got),
             flops=1 << 27,
-            name="restore",
         )
         for i in range(pieces)
     ]

time: 35.2 us -> 35.2 us (level)
  no operation moved by 1% of the time
where the time goes in v3:
time: 35.2 us; the launch traced here: 35 us
  starting transfers between devices  12.1 us (34%)
  waiting for transfers between devices  11 us (31%)
  Pallas kernels  10.8 us (31%)
  other arithmetic  0.89 us (3%)
    pallas_call x9, Pallas kernels, call(): pl.pallas_call(kernel, out_shape=out, in_specs=[spec() for _ in range(len...  10.8 us
    ppermute x6, starting transfers between devices, exchange(): lax.ppermute(values[d - 1], axis, [(i, to(i, d, n)) for i in range(n)])  7.8 us
    ppermute x4, waiting for transfers between devices, body(): others = [lax.ppermute(part, 'member', [(0, 1), (1, 0)]) for part in parts]  7.39 us
    ppermute x4, starting transfers between devices, body(): others = [lax.ppermute(part, 'member', [(0, 1), (1, 0)]) for part in parts]  4.32 us
    ppermute x6, waiting for transfers between devices, exchange(): lax.ppermute(values[d - 1], axis, [(i, to(i, d, n)) for i in range(n)])  3.63 us
    concatenate x1, other arithmetic, body(): return jnp.concatenate([a + b for a, b in zip(parts, others)], 0)  0.83 us
  transfers between devices with their start and end apart: 10, of which 6 were waited for; matrix products, arithmetic and copies ran while one was open for 0% of the time, Pallas kernels for 20%

profile of v3, /device:TPU:0, one launch (start us, length us, event | category | flops | bytes accessed | tf_op | source)
XLA Modules:
  0.0 35.0 jit_solution(15219474233568161568)
XLA Ops:
  0.0 2.8 %shard_map.55 = (f32[1920,128]{1,0:T(8,128)S(1)}, f32[1920,128]{1,0:T(8,128)S(1)}, f32[160,128]{1,0:T(8,128)S(1)}, f32[40,128]{1,0:T(8,128)S(1)}, f32[20,20]{1,0...) custom-call(bf16[2,20,48,128]{3,2,1,0:T(8,128)(2,1)} %p_ref.7, ...), custom_call_target="tpu_custom_call" | custom-call | flops 268435456 | bytes 3300800 | tf_op jit(solution)/shard_map/pallas_call | solution.py:531
  2.8 3.1 %collective-permute-start = (f32[160,128]{1,0:T(8,128)S(1)}, f32[160,128]{1,0:T(8,128)S(1)}, u32[]{:S(2)}, u32[]{:S(2)}) collective-permute-start(f32[160,128]{1,0:T(8,128)S(1)} %get-tuple-element.39), channel_id=1, source_target_pairs={{0,4},{4,0},{8,12},{12,8},{1,5},{5,1},{9,13},{13,9},{2,6},{6,2},{1... | collective-permute-start | bytes 245768 | tf_op jit(solution)/shard_map/ppermute | solution.py:550
  5.9 2.6 %collective-permute-start.1 = (f32[160,128]{1,0:T(8,128)S(1)}, f32[160,128]{1,0:T(8,128)S(1)}, u32[]{:S(2)}, u32[]{:S(2)}) collective-permute-start(f32[160,128]{1,0:T(8,128)S(1)} %get-tuple-element.40), channel_id=1, source_target_pairs={{0,8},{4,12},{8,0},{12,4},{1,9},{5,13},{9,1},{13,5},{2,10},{6,14},... | collective-permute-start | bytes 245768 | tf_op jit(solution)/shard_map/ppermute | solution.py:550
  8.5 0.0 collective-permute-start.2
  8.5 2.6 %shard_map.56 = (f32[128,256]{1,0:T(8,128)S(1)}, bf16[20,128,128]{2,1,0:T(8,128)(2,1)S(1)}, bf16[20,128,128]{2,1,0:T(8,128)(2,1)S(1)}, bf16[768,128]{1,0:T(8,128...) custom-call(f32[20,20]{1,0:T(8,128)S(1)} %get-tuple-element.33.e_ref, f32[1,20]{1,0:T(1,128)S(1)} %get-tuple-element.32.rx_ref, ...), custom_call_target="tpu_custom_call" | custom-call | flops 1073741824 | bytes 1726176 | tf_op jit(solution)/shard_map/pallas_call | solution.py:531
  11.1 1.1 %shard_map.57 = (f32[96,256]{1,0:T(8,128)S(1)}, f32[384,256]{1,0:T(8,128)S(1)}) custom-call(f32[1920,128]{1,0:T(8,128)S(1)} %get-tuple-element.36.z_ref, f32[128,256]{1,0:T(8,128)S(1)} %get-tuple-element.35.send_ref, f32[1,20]{1,0:T(1,128)S(1)} %get-tuple-element.32.rx_ref), custom_call_target="tpu_custom_call" | custom-call | flops 536870912 | bytes 1605712 | tf_op jit(solution)/shard_map/pallas_call | solution.py:531
  12.2 0.0 collective-permute-done.refs_0_
  12.2 2.9 %collective-permute-done.1.refs_1_ = f32[160,128]{1,0:T(8,128)S(1)} collective-permute-done((f32[160,128]{1,0:T(8,128)S(1)}, f32[160,128]{1,0:T(8,128)S(1)}, u32[]{:S(2)}, u32[]{:S(2)}) %collective-permute-start.1) | collective-permute-done | bytes 81952 | tf_op jit(solution)/shard_map/ppermute | solution.py:550
  15.1 0.0 collective-permute-done.2.refs_2_
  15.1 0.5 %shard_map.58 = (f32[320,128]{1,0:T(8,128)S(1)}, f32[96,128]{1,0:T(8,128)S(1)}, f32[96,128]{1,0:T(8,128)S(1)}, f32[96,128]{1,0:T(8,128)S(1)}) custom-call(f32[160,128]{1,0:T(8,128)S(1)} %get-tuple-element.30.end_ref, f32[40,128]{1,0:T(8,128)S(1)} %get-tuple-element.31.hat_ref, f32[1,20]{1,0:T(1,128)S(1)} %get-tuple-element.32.rx_ref, ...), custom_call_target="tpu_custom_call" | custom-call | flops 134217728 | bytes 1282128 | tf_op jit(solution)/shard_map/pallas_call | solution.py:531
  15.7 1.6 %collective-permute-start.4 = (f32[96,128]{1,0:T(8,128)S(1)}, f32[96,128]{1,0:T(8,128)S(1)}, u32[]{:S(2)}, u32[]{:S(2)}) collective-permute-start(f32[96,128]{1,0:T(8,128)S(1)} %get-tuple-element.51), channel_id=1, source_target_pairs={{0,2},{1,3},{2,0},{3,1},{4,6},{5,7},{6,4},{7,5},{8,10},{9,11},{10,... | collective-permute-start | bytes 147464 | tf_op jit(solution)/shard_map/ppermute | solution.py:550
  17.2 0.0 collective-permute-start.5
  17.2 0.5 %collective-permute-start.3 = (f32[96,128]{1,0:T(8,128)S(1)}, f32[96,128]{1,0:T(8,128)S(1)}, u32[]{:S(2)}, u32[]{:S(2)}) collective-permute-start(f32[96,128]{1,0:T(8,128)S(1)} %get-tuple-element.45.sent_ref), channel_id=1, source_target_pairs={{0,1},{1,2},{2,3},{3,0},{4,5},{5,6},{6,7},{7,4},{8,9},{9,10},{10,1... | collective-permute-start | bytes 147464 | tf_op jit(solution)/shard_map/ppermute | solution.py:550
  17.8 0.0 copy-start
  17.8 2.4 %shard_map.59 = (f32[40,48,128]{2,1,0:T(8,128)S(1)}, f32[96,128]{1,0:T(8,128)S(1)}) custom-call(f32[1920,128]{1,0:T(8,128)S(1)} %get-tuple-element.29.proj_ref, f32[320,128]{1,0:T(8,128)S(1)} %get-tuple-element.42.enter_ref, bf16[20,128,128]{2,1,0:T(8,128)(2,1)S(1)} %get-tuple-element.43.high_ref, bf16[20,128,128]{2,1,0:T(8,128)(2,1)S(1)} %get-tuple-element.44.low_ref, ...), custom_call_target="tpu_custom_call" | custom-call | flops 536870912 | bytes 3606240 | tf_op jit(solution)/shard_map/pallas_call | solution.py:531
  20.1 0.0 collective-permute-done.4.refs_1_
  20.1 0.0 collective-permute-done.5.refs_2_
  20.2 0.7 %collective-permute-done.3.refs_0_ = f32[96,128]{1,0:T(8,128)S(1)} collective-permute-done((f32[96,128]{1,0:T(8,128)S(1)}, f32[96,128]{1,0:T(8,128)S(1)}, u32[]{:S(2)}, u32[]{:S(2)}) %collective-permute-start.3) | collective-permute-done | bytes 49184 | tf_op jit(solution)/shard_map/ppermute | solution.py:550
  20.9 0.0 copy-done
  20.9 0.4 %shard_map.60 = f32[5,48,128]{2,1,0:T(8,128)S(1)} custom-call(bf16[2,20,48,128]{3,2,1,0:T(8,128)(2,1)S(1)} %copy-done, f32[40,48,128]{2,1,0:T(8,128)S(1)} %get-tuple-element.47.base_ref, f32[96,128]{1,0:T(8,128)S(1)} %get-tuple-element.48.right_ref, bf16[768,128]{1,0:T(8,128)(2,1)S(1)} %get-tuple-element.49.fix_ref, ...), custom_call_target="tpu_custom_call" | custom-call | flops 134217728 | bytes 2011136 | tf_op jit(solution)/shard_map/pallas_call | solution.py:531
  21.2 1.6 %collective-permute-start.6 = (f32[5,48,128]{2,1,0:T(8,128)S(1)}, f32[5,48,128]{2,1,0:T(8,128)S(1)}, u32[]{:S(2)}, u32[]{:S(2)}) collective-permute-start(f32[5,48,128]{2,1,0:T(8,128)S(1)} %shard_map.60), channel_id=1, source_target_pairs={{0,16},{16,0},{1,17},{17,1},{2,18},{18,2},{3,19},{19,3},{4,20},{20... | collective-permute-start | bytes 368648 | tf_op jit(solution)/shard_map/ppermute | solution.py:639
  22.8 0.4 %shard_map.61 = f32[5,48,128]{2,1,0:T(8,128)S(1)} custom-call(bf16[2,20,48,128]{3,2,1,0:T(8,128)(2,1)S(1)} %copy-done, f32[40,48,128]{2,1,0:T(8,128)S(1)} %get-tuple-element.47.base_ref, f32[96,128]{1,0:T(8,128)S(1)} %get-tuple-element.48.right_ref, bf16[768,128]{1,0:T(8,128)(2,1)S(1)} %get-tuple-element.49.fix_ref, ...), custom_call_target="tpu_custom_call" | custom-call | flops 134217728 | bytes 2011136 | tf_op jit(solution)/shard_map/pallas_call | solution.py:531
  23.2 0.6 %collective-permute-start.7 = (f32[5,48,128]{2,1,0:T(8,128)S(1)}, f32[5,48,128]{2,1,0:T(8,128)S(1)}, u32[]{:S(2)}, u32[]{:S(2)}) collective-permute-start(f32[5,48,128]{2,1,0:T(8,128)S(1)} %shard_map.61), channel_id=1, source_target_pairs={{0,16},{16,0},{1,17},{17,1},{2,18},{18,2},{3,19},{19,3},{4,20},{20... | collective-permute-start | bytes 368648 | tf_op jit(solution)/shard_map/ppermute | solution.py:639
  23.8 0.4 %shard_map.62 = f32[5,48,128]{2,1,0:T(8,128)S(1)} custom-call(bf16[2,20,48,128]{3,2,1,0:T(8,128)(2,1)S(1)} %copy-done, f32[40,48,128]{2,1,0:T(8,128)S(1)} %get-tuple-element.47.base_ref, f32[96,128]{1,0:T(8,128)S(1)} %get-tuple-element.48.right_ref, bf16[768,128]{1,0:T(8,128)(2,1)S(1)} %get-tuple-element.49.fix_ref, ...), custom_call_target="tpu_custom_call" | custom-call | flops 134217728 | bytes 2011136 | tf_op jit(solution)/shard_map/pallas_call | solution.py:531
  24.1 1.6 %collective-permute-start.8 = (f32[5,48,128]{2,1,0:T(8,128)S(1)}, f32[5,48,128]{2,1,0:T(8,128)S(1)}, u32[]{:S(2)}, u32[]{:S(2)}) collective-permute-start(f32[5,48,128]{2,1,0:T(8,128)S(1)} %shard_map.62), channel_id=1, source_target_pairs={{0,16},{16,0},{1,17},{17,1},{2,18},{18,2},{3,19},{19,3},{4,20},{20... | collective-permute-start | bytes 368648 | tf_op jit(solution)/shard_map/ppermute | solution.py:639
  25.7 0.4 %shard_map.63 = f32[5,48,128]{2,1,0:T(8,128)S(1)} custom-call(bf16[2,20,48,128]{3,2,1,0:T(8,128)(2,1)S(1)} %copy-done, f32[40,48,128]{2,1,0:T(8,128)S(1)} %get-tuple-element.47.base_ref, f32[96,128]{1,0:T(8,128)S(1)} %get-tuple-element.48.right_ref, bf16[768,128]{1,0:T(8,128)(2,1)S(1)} %get-tuple-element.49.fix_ref, ...), custom_call_target="tpu_custom_call" | custom-call | flops 134217728 | bytes 2011136 | tf_op jit(solution)/shard_map/pallas_call | solution.py:531
  26.1 0.6 %collective-permute-start.9 = (f32[5,48,128]{2,1,0:T(8,128)S(1)}, f32[5,48,128]{2,1,0:T(8,128)S(1)}, u32[]{:S(2)}, u32[]{:S(2)}) collective-permute-start(f32[5,48,128]{2,1,0:T(8,128)S(1)} %shard_map.63), channel_id=1, source_target_pairs={{0,16},{16,0},{1,17},{17,1},{2,18},{18,2},{3,19},{19,3},{4,20},{20... | collective-permute-start | bytes 368648 | tf_op jit(solution)/shard_map/ppermute | solution.py:639
  26.7 0.5 %collective-permute-done.6 = f32[5,48,128]{2,1,0:T(8,128)S(1)} collective-permute-done((f32[5,48,128]{2,1,0:T(8,128)S(1)}, f32[5,48,128]{2,1,0:T(8,128)S(1)}, u32[]{:S(2)}, u32[]{:S(2)}) %collective-permute-start.6) | collective-permute-done | bytes 122912 | tf_op jit(solution)/shard_map/ppermute | solution.py:639
  27.2 2.6 %collective-permute-done.7 = f32[5,48,128]{2,1,0:T(8,128)S(1)} collective-permute-done((f32[5,48,128]{2,1,0:T(8,128)S(1)}, f32[5,48,128]{2,1,0:T(8,128)S(1)}, u32[]{:S(2)}, u32[]{:S(2)}) %collective-permute-start.7) | collective-permute-done | bytes 122912 | tf_op jit(solution)/shard_map/ppermute | solution.py:639
  29.8 2.6 %collective-permute-done.8 = f32[5,48,128]{2,1,0:T(8,128)S(1)} collective-permute-done((f32[5,48,128]{2,1,0:T(8,128)S(1)}, f32[5,48,128]{2,1,0:T(8,128)S(1)}, u32[]{:S(2)}, u32[]{:S(2)}) %collective-permute-start.8) | collective-permute-done | bytes 122912 | tf_op jit(solution)/shard_map/ppermute | solution.py:639
  32.5 1.7 %collective-permute-done.9 = f32[5,48,128]{2,1,0:T(8,128)S(1)} collective-permute-done((f32[5,48,128]{2,1,0:T(8,128)S(1)}, f32[5,48,128]{2,1,0:T(8,128)S(1)}, u32[]{:S(2)}, u32[]{:S(2)}) %collective-permute-start.9) | collective-permute-done | bytes 122912 | tf_op jit(solution)/shard_map/ppermute | solution.py:639
  34.1 0.8 %pad_maximum_fusion = f32[20,48,128]{2,1,0:T(8,128)} fusion(f32[5,48,128]{2,1,0:T(8,128)S(1)} %add.15, f32[5,48,128]{2,1,0:T(8,128)S(1)} %add.14, f32[5,48,128]{2,1,0:T(8,128)S(1)} %add.13, f32[5,48,128]{2,1,0:T(8,128)S(1)} %add.12), kind=kLoop, calls=%fused_computation | loop fusion | flops 368640 | bytes 983040 | tf_op jit(solution)/shard_map/concatenate | solution.py:640
  (4 shorter events, 0.1 us)
Async XLA Ops:
  2.8 9.4 %collective-permute-start = (f32[160,128]{1,0:T(8,128)S(1)}, f32[160,128]{1,0:T(8,128)S(1)}, u32[]{:S(2)}, u32[]{:S(2)}) collective-permute-start(f32[160,128]{1,0:T(8,128)S(1)} %get-tuple-element.39), channel_id=1, source_target_pairs={{0,4},{4,0},{8,12},{12,8},{1,5},{5,1},{9,13},{13,9},{2,6},{6,2},{1... | collective-permute-start | bytes 245768 | tf_op jit(solution)/shard_map/ppermute | solution.py:550
  5.9 9.2 %collective-permute-start.1 = (f32[160,128]{1,0:T(8,128)S(1)}, f32[160,128]{1,0:T(8,128)S(1)}, u32[]{:S(2)}, u32[]{:S(2)}) collective-permute-start(f32[160,128]{1,0:T(8,128)S(1)} %get-tuple-element.40), channel_id=1, source_target_pairs={{0,8},{4,12},{8,0},{12,4},{1,9},{5,13},{9,1},{13,5},{2,10},{6,14},... | collective-permute-start | bytes 245768 | tf_op jit(solution)/shard_map/ppermute | solution.py:550
  8.5 6.6 %collective-permute-start.2 = (f32[160,128]{1,0:T(8,128)S(1)}, f32[160,128]{1,0:T(8,128)S(1)}, u32[]{:S(2)}, u32[]{:S(2)}) collective-permute-start(f32[160,128]{1,0:T(8,128)S(1)} %get-tuple-element.41), channel_id=1, source_target_pairs={{0,12},{4,8},{8,4},{12,0},{1,13},{5,9},{9,5},{13,1},{2,14},{6,10},... | collective-permute-start | bytes 245768 | tf_op jit(solution)/shard_map/ppermute | solution.py:550
  15.7 4.5 %collective-permute-start.4 = (f32[96,128]{1,0:T(8,128)S(1)}, f32[96,128]{1,0:T(8,128)S(1)}, u32[]{:S(2)}, u32[]{:S(2)}) collective-permute-start(f32[96,128]{1,0:T(8,128)S(1)} %get-tuple-element.51), channel_id=1, source_target_pairs={{0,2},{1,3},{2,0},{3,1},{4,6},{5,7},{6,4},{7,5},{8,10},{9,11},{10,... | collective-permute-start | bytes 147464 | tf_op jit(solution)/shard_map/ppermute | solution.py:550
  17.2 2.9 %collective-permute-start.5 = (f32[96,128]{1,0:T(8,128)S(1)}, f32[96,128]{1,0:T(8,128)S(1)}, u32[]{:S(2)}, u32[]{:S(2)}) collective-permute-start(f32[96,128]{1,0:T(8,128)S(1)} %get-tuple-element.52), channel_id=1, source_target_pairs={{0,3},{1,0},{2,1},{3,2},{4,7},{5,4},{6,5},{7,6},{8,11},{9,8},{10,9... | collective-permute-start | bytes 147464 | tf_op jit(solution)/shard_map/ppermute | solution.py:550
  17.2 3.6 %collective-permute-start.3 = (f32[96,128]{1,0:T(8,128)S(1)}, f32[96,128]{1,0:T(8,128)S(1)}, u32[]{:S(2)}, u32[]{:S(2)}) collective-permute-start(f32[96,128]{1,0:T(8,128)S(1)} %get-tuple-element.45.sent_ref), channel_id=1, source_target_pairs={{0,1},{1,2},{2,3},{3,0},{4,5},{5,6},{6,7},{7,4},{8,9},{9,10},{10,1... | collective-permute-start | bytes 147464 | tf_op jit(solution)/shard_map/ppermute | solution.py:550
  17.8 3.1 %copy-start = (bf16[2,20,48,128]{3,2,1,0:T(8,128)(2,1)S(1)}, bf16[2,20,48,128]{3,2,1,0:T(8,128)(2,1)}, u32[]{:S(2)}) copy-start(bf16[2,20,48,128]{3,2,1,0:T(8,128)(2,1)} %p_ref.7) | copy-start | bytes 1474564
  21.2 5.9 %collective-permute-start.6 = (f32[5,48,128]{2,1,0:T(8,128)S(1)}, f32[5,48,128]{2,1,0:T(8,128)S(1)}, u32[]{:S(2)}, u32[]{:S(2)}) collective-permute-start(f32[5,48,128]{2,1,0:T(8,128)S(1)} %shard_map.60), channel_id=1, source_target_pairs={{0,16},{16,0},{1,17},{17,1},{2,18},{18,2},{3,19},{19,3},{4,20},{20... | collective-permute-start | bytes 368648 | tf_op jit(solution)/shard_map/ppermute | solution.py:639
  23.2 6.6 %collective-permute-start.7 = (f32[5,48,128]{2,1,0:T(8,128)S(1)}, f32[5,48,128]{2,1,0:T(8,128)S(1)}, u32[]{:S(2)}, u32[]{:S(2)}) collective-permute-start(f32[5,48,128]{2,1,0:T(8,128)S(1)} %shard_map.61), channel_id=1, source_target_pairs={{0,16},{16,0},{1,17},{17,1},{2,18},{18,2},{3,19},{19,3},{4,20},{20... | collective-permute-start | bytes 368648 | tf_op jit(solution)/shard_map/ppermute | solution.py:639
  24.1 8.3 %collective-permute-start.8 = (f32[5,48,128]{2,1,0:T(8,128)S(1)}, f32[5,48,128]{2,1,0:T(8,128)S(1)}, u32[]{:S(2)}, u32[]{:S(2)}) collective-permute-start(f32[5,48,128]{2,1,0:T(8,128)S(1)} %shard_map.62), channel_id=1, source_target_pairs={{0,16},{16,0},{1,17},{17,1},{2,18},{18,2},{3,19},{19,3},{4,20},{20... | collective-permute-start | bytes 368648 | tf_op jit(solution)/shard_map/ppermute | solution.py:639
  26.1 8.0 %collective-permute-start.9 = (f32[5,48,128]{2,1,0:T(8,128)S(1)}, f32[5,48,128]{2,1,0:T(8,128)S(1)}, u32[]{:S(2)}, u32[]{:S(2)}) collective-permute-start(f32[5,48,128]{2,1,0:T(8,128)S(1)} %shard_map.63), channel_id=1, source_target_pairs={{0,16},{16,0},{1,17},{17,1},{2,18},{18,2},{3,19},{19,3},{4,20},{20... | collective-permute-start | bytes 368648 | tf_op jit(solution)/shard_map/ppermute | solution.py:639

commit v4 on v3

--- a/solution.py
+++ b/solution.py
@@ -64,11 +64,14 @@
 
 
 def expanded(matrix, rows, cols):
-    left = (iota((rows * SUB, rows), 0) // SUB == iota((rows * SUB, rows), 1)).astype(F32)
-    right = (iota((cols, cols * SUB), 1) // SUB == iota((cols, cols * SUB), 0)).astype(F32)
-    full = exact(exact(left, matrix), right)
+    left = (iota((rows * SUB, rows), 0) // SUB == iota((rows * SUB, rows), 1)).astype(BF16)
+    right = (iota((cols, cols * SUB), 1) // SUB == iota((cols, cols * SUB), 0)).astype(BF16)
     shape = (rows * SUB, cols * SUB)
-    return jnp.where(iota(shape, 0) % SUB == iota(shape, 1) % SUB, full, 0.0)
+    own = iota(shape, 0) % SUB == iota(shape, 1) % SUB
+    return [
+        jnp.where(own, dot(dot(left, part).astype(BF16), right), 0.0).astype(BF16)
+        for part in split(matrix)
+    ]
 
 
 def shifted(coefficients, states):
@@ -123,9 +126,8 @@
     rate = rx_ref[...]
     pitch = n_ref.shape[0] // rows
 
-    z_rows = column_of(rate, lambda i: i // SUB, modes * SUB) * (1.0 / extent)
-    g_rows = gain(z_rows)
-    mix = split(expanded(e_ref[...].T, modes, levels) * (g_rows * g_rows) * (g_rows * g_rows))
+    g_rows = gain(column_of(rate, lambda i: i, modes) * (1.0 / extent))
+    mix = expanded(e_ref[...].T * ((g_rows * g_rows) * (g_rows * g_rows)), modes, levels)
     mix_ref[...] = jnp.concatenate([mix[0], mix[0], mix[1]], 1)
 
     z = column_of(rate, lambda i: i % modes, rows) * (1.0 / extent)
@@ -480,7 +482,7 @@
     gx = gain(rx_ref[...] * (1.0 / extent_x))
     pass_gain = (g * g) * (g * g)
     scale = jnp.sqrt((2.0 - g) / g) * jnp.sqrt((2.0 - gx) / gx) * pass_gain * pass_gain
-    mix = split(expanded(e_ref[...] * scale, levels, modes))
+    mix = expanded(e_ref[...] * scale, levels, modes)
     for t in range(nx // SUB):
         wide = jnp.concatenate(
             [

time: 35.2 us -> 34.9 us (level)
  Pallas kernels: 10.8 us -> 10.2 us
  waiting for transfers between devices: 11 us -> 11.5 us
    pallas_call x9, Pallas kernels: 10.8 us -> 10.2 us  [call(): pl.pallas_call(kernel, out_shape=out, in_specs=[spec() for _ in range(len...]
    ppermute x6, waiting for transfers between devices: 3.63 us -> 4.06 us  [exchange(): lax.ppermute(values[d - 1], axis, [(i, to(i, d, n)) for i in range(n)])]
  transfers between devices with their start and end apart: 10 -> 10, of which waited for: 6 -> 7; matrix products, arithmetic and copies ran while one was open for 0% -> 0% of each run, Pallas kernels for 20% -> 19%
where the time goes in v4:
time: 34.9 us; the launch traced here: 34.7 us
  starting transfers between devices  12.1 us (35%)
  waiting for transfers between devices  11.5 us (33%)
  Pallas kernels  10.2 us (29%)
  other arithmetic  0.89 us (3%)
    pallas_call x9, Pallas kernels, call(): pl.pallas_call(kernel, out_shape=out, in_specs=[spec() for _ in range(len...  10.2 us
    ppermute x6, starting transfers between devices, exchange(): lax.ppermute(values[d - 1], axis, [(i, to(i, d, n)) for i in range(n)])  7.8 us
    ppermute x4, waiting for transfers between devices, body(): others = [lax.ppermute(part, 'member', [(0, 1), (1, 0)]) for part in parts]  7.41 us
    ppermute x4, starting transfers between devices, body(): others = [lax.ppermute(part, 'member', [(0, 1), (1, 0)]) for part in parts]  4.29 us
    ppermute x6, waiting for transfers between devices, exchange(): lax.ppermute(values[d - 1], axis, [(i, to(i, d, n)) for i in range(n)])  4.06 us
    concatenate x1, other arithmetic, body(): return jnp.concatenate([a + b for a, b in zip(parts, others)], 0)  0.83 us
  transfers between devices with their start and end apart: 10, of which 7 were waited for; matrix products, arithmetic and copies ran while one was open for 0% of the time, Pallas kernels for 19%

profile of v4, /device:TPU:0, one launch (start us, length us, event | category | flops | bytes accessed | tf_op | source)
XLA Modules:
  0.0 34.7 jit_solution(11598680441697756709)
XLA Ops:
  0.0 2.5 %shard_map.55 = (f32[1920,128]{1,0:T(8,128)S(1)}, f32[1920,128]{1,0:T(8,128)S(1)}, f32[160,128]{1,0:T(8,128)S(1)}, f32[40,128]{1,0:T(8,128)S(1)}, f32[20,20]{1,0...) custom-call(bf16[2,20,48,128]{3,2,1,0:T(8,128)(2,1)} %p_ref.7, ...), custom_call_target="tpu_custom_call" | custom-call | flops 268435456 | bytes 3300800 | tf_op jit(solution)/shard_map/pallas_call | solution.py:533
  2.5 3.1 %collective-permute-start = (f32[160,128]{1,0:T(8,128)S(1)}, f32[160,128]{1,0:T(8,128)S(1)}, u32[]{:S(2)}, u32[]{:S(2)}) collective-permute-start(f32[160,128]{1,0:T(8,128)S(1)} %get-tuple-element.39), channel_id=1, source_target_pairs={{0,4},{4,0},{8,12},{12,8},{1,5},{5,1},{9,13},{13,9},{2,6},{6,2},{1... | collective-permute-start | bytes 245768 | tf_op jit(solution)/shard_map/ppermute | solution.py:552
  5.7 2.6 %collective-permute-start.1 = (f32[160,128]{1,0:T(8,128)S(1)}, f32[160,128]{1,0:T(8,128)S(1)}, u32[]{:S(2)}, u32[]{:S(2)}) collective-permute-start(f32[160,128]{1,0:T(8,128)S(1)} %get-tuple-element.40), channel_id=1, source_target_pairs={{0,8},{4,12},{8,0},{12,4},{1,9},{5,13},{9,1},{13,5},{2,10},{6,14},... | collective-permute-start | bytes 245768 | tf_op jit(solution)/shard_map/ppermute | solution.py:552
  8.3 0.0 collective-permute-start.2
  8.3 2.6 %shard_map.56 = (f32[128,256]{1,0:T(8,128)S(1)}, bf16[20,128,128]{2,1,0:T(8,128)(2,1)S(1)}, bf16[20,128,128]{2,1,0:T(8,128)(2,1)S(1)}, bf16[768,128]{1,0:T(8,128...) custom-call(f32[20,20]{1,0:T(8,128)S(1)} %get-tuple-element.33.e_ref, f32[1,20]{1,0:T(1,128)S(1)} %get-tuple-element.32.rx_ref, ...), custom_call_target="tpu_custom_call" | custom-call | flops 1073741824 | bytes 1726176 | tf_op jit(solution)/shard_map/pallas_call | solution.py:533
  10.8 1.1 %shard_map.57 = (f32[96,256]{1,0:T(8,128)S(1)}, f32[384,256]{1,0:T(8,128)S(1)}) custom-call(f32[1920,128]{1,0:T(8,128)S(1)} %get-tuple-element.36.z_ref, f32[128,256]{1,0:T(8,128)S(1)} %get-tuple-element.35.send_ref, f32[1,20]{1,0:T(1,128)S(1)} %get-tuple-element.32.rx_ref), custom_call_target="tpu_custom_call" | custom-call | flops 536870912 | bytes 1605712 | tf_op jit(solution)/shard_map/pallas_call | solution.py:533
  11.9 0.0 collective-permute-done.refs_0_
  11.9 2.9 %collective-permute-done.1.refs_1_ = f32[160,128]{1,0:T(8,128)S(1)} collective-permute-done((f32[160,128]{1,0:T(8,128)S(1)}, f32[160,128]{1,0:T(8,128)S(1)}, u32[]{:S(2)}, u32[]{:S(2)}) %collective-permute-start.1) | collective-permute-done | bytes 81952 | tf_op jit(solution)/shard_map/ppermute | solution.py:552
  14.9 0.0 collective-permute-done.2.refs_2_
  14.9 0.5 %shard_map.58 = (f32[320,128]{1,0:T(8,128)S(1)}, f32[96,128]{1,0:T(8,128)S(1)}, f32[96,128]{1,0:T(8,128)S(1)}, f32[96,128]{1,0:T(8,128)S(1)}) custom-call(f32[160,128]{1,0:T(8,128)S(1)} %get-tuple-element.30.end_ref, f32[40,128]{1,0:T(8,128)S(1)} %get-tuple-element.31.hat_ref, f32[1,20]{1,0:T(1,128)S(1)} %get-tuple-element.32.rx_ref, ...), custom_call_target="tpu_custom_call" | custom-call | flops 134217728 | bytes 1282128 | tf_op jit(solution)/shard_map/pallas_call | solution.py:533
  15.4 1.6 %collective-permute-start.4 = (f32[96,128]{1,0:T(8,128)S(1)}, f32[96,128]{1,0:T(8,128)S(1)}, u32[]{:S(2)}, u32[]{:S(2)}) collective-permute-start(f32[96,128]{1,0:T(8,128)S(1)} %get-tuple-element.51), channel_id=1, source_target_pairs={{0,2},{1,3},{2,0},{3,1},{4,6},{5,7},{6,4},{7,5},{8,10},{9,11},{10,... | collective-permute-start | bytes 147464 | tf_op jit(solution)/shard_map/ppermute | solution.py:552
  17.0 0.0 collective-permute-start.5
  17.0 0.5 %collective-permute-start.3 = (f32[96,128]{1,0:T(8,128)S(1)}, f32[96,128]{1,0:T(8,128)S(1)}, u32[]{:S(2)}, u32[]{:S(2)}) collective-permute-start(f32[96,128]{1,0:T(8,128)S(1)} %get-tuple-element.45.sent_ref), channel_id=1, source_target_pairs={{0,1},{1,2},{2,3},{3,0},{4,5},{5,6},{6,7},{7,4},{8,9},{9,10},{10,1... | collective-permute-start | bytes 147464 | tf_op jit(solution)/shard_map/ppermute | solution.py:552
  17.5 0.0 copy-start
  17.5 2.0 %shard_map.59 = (f32[40,48,128]{2,1,0:T(8,128)S(1)}, f32[96,128]{1,0:T(8,128)S(1)}) custom-call(f32[1920,128]{1,0:T(8,128)S(1)} %get-tuple-element.29.proj_ref, f32[320,128]{1,0:T(8,128)S(1)} %get-tuple-element.42.enter_ref, bf16[20,128,128]{2,1,0:T(8,128)(2,1)S(1)} %get-tuple-element.43.high_ref, bf16[20,128,128]{2,1,0:T(8,128)(2,1)S(1)} %get-tuple-element.44.low_ref, ...), custom_call_target="tpu_custom_call" | custom-call | flops 536870912 | bytes 3606240 | tf_op jit(solution)/shard_map/pallas_call | solution.py:533
  19.5 0.1 collective-permute-done.4.refs_1_
  19.6 0.0 collective-permute-done.5.refs_2_
  19.6 1.0 %collective-permute-done.3.refs_0_ = f32[96,128]{1,0:T(8,128)S(1)} collective-permute-done((f32[96,128]{1,0:T(8,128)S(1)}, f32[96,128]{1,0:T(8,128)S(1)}, u32[]{:S(2)}, u32[]{:S(2)}) %collective-permute-start.3) | collective-permute-done | bytes 49184 | tf_op jit(solution)/shard_map/ppermute | solution.py:552
  20.6 0.0 copy-done
  20.6 0.4 %shard_map.60 = f32[5,48,128]{2,1,0:T(8,128)S(1)} custom-call(bf16[2,20,48,128]{3,2,1,0:T(8,128)(2,1)S(1)} %copy-done, f32[40,48,128]{2,1,0:T(8,128)S(1)} %get-tuple-element.47.base_ref, f32[96,128]{1,0:T(8,128)S(1)} %get-tuple-element.48.right_ref, bf16[768,128]{1,0:T(8,128)(2,1)S(1)} %get-tuple-element.49.fix_ref, ...), custom_call_target="tpu_custom_call" | custom-call | flops 134217728 | bytes 2011136 | tf_op jit(solution)/shard_map/pallas_call | solution.py:533
  21.0 1.6 %collective-permute-start.6 = (f32[5,48,128]{2,1,0:T(8,128)S(1)}, f32[5,48,128]{2,1,0:T(8,128)S(1)}, u32[]{:S(2)}, u32[]{:S(2)}) collective-permute-start(f32[5,48,128]{2,1,0:T(8,128)S(1)} %shard_map.60), channel_id=1, source_target_pairs={{0,16},{16,0},{1,17},{17,1},{2,18},{18,2},{3,19},{19,3},{4,20},{20... | collective-permute-start | bytes 368648 | tf_op jit(solution)/shard_map/ppermute | solution.py:641
  22.6 0.4 %shard_map.61 = f32[5,48,128]{2,1,0:T(8,128)S(1)} custom-call(bf16[2,20,48,128]{3,2,1,0:T(8,128)(2,1)S(1)} %copy-done, f32[40,48,128]{2,1,0:T(8,128)S(1)} %get-tuple-element.47.base_ref, f32[96,128]{1,0:T(8,128)S(1)} %get-tuple-element.48.right_ref, bf16[768,128]{1,0:T(8,128)(2,1)S(1)} %get-tuple-element.49.fix_ref, ...), custom_call_target="tpu_custom_call" | custom-call | flops 134217728 | bytes 2011136 | tf_op jit(solution)/shard_map/pallas_call | solution.py:533
  22.9 0.6 %collective-permute-start.7 = (f32[5,48,128]{2,1,0:T(8,128)S(1)}, f32[5,48,128]{2,1,0:T(8,128)S(1)}, u32[]{:S(2)}, u32[]{:S(2)}) collective-permute-start(f32[5,48,128]{2,1,0:T(8,128)S(1)} %shard_map.61), channel_id=1, source_target_pairs={{0,16},{16,0},{1,17},{17,1},{2,18},{18,2},{3,19},{19,3},{4,20},{20... | collective-permute-start | bytes 368648 | tf_op jit(solution)/shard_map/ppermute | solution.py:641
  23.5 0.4 %shard_map.62 = f32[5,48,128]{2,1,0:T(8,128)S(1)} custom-call(bf16[2,20,48,128]{3,2,1,0:T(8,128)(2,1)S(1)} %copy-done, f32[40,48,128]{2,1,0:T(8,128)S(1)} %get-tuple-element.47.base_ref, f32[96,128]{1,0:T(8,128)S(1)} %get-tuple-element.48.right_ref, bf16[768,128]{1,0:T(8,128)(2,1)S(1)} %get-tuple-element.49.fix_ref, ...), custom_call_target="tpu_custom_call" | custom-call | flops 134217728 | bytes 2011136 | tf_op jit(solution)/shard_map/pallas_call | solution.py:533
  23.9 1.6 %collective-permute-start.8 = (f32[5,48,128]{2,1,0:T(8,128)S(1)}, f32[5,48,128]{2,1,0:T(8,128)S(1)}, u32[]{:S(2)}, u32[]{:S(2)}) collective-permute-start(f32[5,48,128]{2,1,0:T(8,128)S(1)} %shard_map.62), channel_id=1, source_target_pairs={{0,16},{16,0},{1,17},{17,1},{2,18},{18,2},{3,19},{19,3},{4,20},{20... | collective-permute-start | bytes 368648 | tf_op jit(solution)/shard_map/ppermute | solution.py:641
  25.5 0.4 %shard_map.63 = f32[5,48,128]{2,1,0:T(8,128)S(1)} custom-call(bf16[2,20,48,128]{3,2,1,0:T(8,128)(2,1)S(1)} %copy-done, f32[40,48,128]{2,1,0:T(8,128)S(1)} %get-tuple-element.47.base_ref, f32[96,128]{1,0:T(8,128)S(1)} %get-tuple-element.48.right_ref, bf16[768,128]{1,0:T(8,128)(2,1)S(1)} %get-tuple-element.49.fix_ref, ...), custom_call_target="tpu_custom_call" | custom-call | flops 134217728 | bytes 2011136 | tf_op jit(solution)/shard_map/pallas_call | solution.py:533
  25.8 0.6 %collective-permute-start.9 = (f32[5,48,128]{2,1,0:T(8,128)S(1)}, f32[5,48,128]{2,1,0:T(8,128)S(1)}, u32[]{:S(2)}, u32[]{:S(2)}) collective-permute-start(f32[5,48,128]{2,1,0:T(8,128)S(1)} %shard_map.63), channel_id=1, source_target_pairs={{0,16},{16,0},{1,17},{17,1},{2,18},{18,2},{3,19},{19,3},{4,20},{20... | collective-permute-start | bytes 368648 | tf_op jit(solution)/shard_map/ppermute | solution.py:641
  26.4 0.6 %collective-permute-done.6 = f32[5,48,128]{2,1,0:T(8,128)S(1)} collective-permute-done((f32[5,48,128]{2,1,0:T(8,128)S(1)}, f32[5,48,128]{2,1,0:T(8,128)S(1)}, u32[]{:S(2)}, u32[]{:S(2)}) %collective-permute-start.6) | collective-permute-done | bytes 122912 | tf_op jit(solution)/shard_map/ppermute | solution.py:641
  27.0 2.6 %collective-permute-done.7 = f32[5,48,128]{2,1,0:T(8,128)S(1)} collective-permute-done((f32[5,48,128]{2,1,0:T(8,128)S(1)}, f32[5,48,128]{2,1,0:T(8,128)S(1)}, u32[]{:S(2)}, u32[]{:S(2)}) %collective-permute-start.7) | collective-permute-done | bytes 122912 | tf_op jit(solution)/shard_map/ppermute | solution.py:641
  29.6 2.6 %collective-permute-done.8 = f32[5,48,128]{2,1,0:T(8,128)S(1)} collective-permute-done((f32[5,48,128]{2,1,0:T(8,128)S(1)}, f32[5,48,128]{2,1,0:T(8,128)S(1)}, u32[]{:S(2)}, u32[]{:S(2)}) %collective-permute-start.8) | collective-permute-done | bytes 122912 | tf_op jit(solution)/shard_map/ppermute | solution.py:641
  32.2 1.6 %collective-permute-done.9 = f32[5,48,128]{2,1,0:T(8,128)S(1)} collective-permute-done((f32[5,48,128]{2,1,0:T(8,128)S(1)}, f32[5,48,128]{2,1,0:T(8,128)S(1)}, u32[]{:S(2)}, u32[]{:S(2)}) %collective-permute-start.9) | collective-permute-done | bytes 122912 | tf_op jit(solution)/shard_map/ppermute | solution.py:641
  33.9 0.8 %pad_maximum_fusion = f32[20,48,128]{2,1,0:T(8,128)} fusion(f32[5,48,128]{2,1,0:T(8,128)S(1)} %add.15, f32[5,48,128]{2,1,0:T(8,128)S(1)} %add.14, f32[5,48,128]{2,1,0:T(8,128)S(1)} %add.13, f32[5,48,128]{2,1,0:T(8,128)S(1)} %add.12), kind=kLoop, calls=%fused_computation | loop fusion | flops 368640 | bytes 983040 | tf_op jit(solution)/shard_map/concatenate | solution.py:642
  (4 shorter events, 0.1 us)
Async XLA Ops:
  2.5 9.4 %collective-permute-start = (f32[160,128]{1,0:T(8,128)S(1)}, f32[160,128]{1,0:T(8,128)S(1)}, u32[]{:S(2)}, u32[]{:S(2)}) collective-permute-start(f32[160,128]{1,0:T(8,128)S(1)} %get-tuple-element.39), channel_id=1, source_target_pairs={{0,4},{4,0},{8,12},{12,8},{1,5},{5,1},{9,13},{13,9},{2,6},{6,2},{1... | collective-permute-start | bytes 245768 | tf_op jit(solution)/shard_map/ppermute | solution.py:552
  5.7 9.2 %collective-permute-start.1 = (f32[160,128]{1,0:T(8,128)S(1)}, f32[160,128]{1,0:T(8,128)S(1)}, u32[]{:S(2)}, u32[]{:S(2)}) collective-permute-start(f32[160,128]{1,0:T(8,128)S(1)} %get-tuple-element.40), channel_id=1, source_target_pairs={{0,8},{4,12},{8,0},{12,4},{1,9},{5,13},{9,1},{13,5},{2,10},{6,14},... | collective-permute-start | bytes 245768 | tf_op jit(solution)/shard_map/ppermute | solution.py:552
  8.3 6.6 %collective-permute-start.2 = (f32[160,128]{1,0:T(8,128)S(1)}, f32[160,128]{1,0:T(8,128)S(1)}, u32[]{:S(2)}, u32[]{:S(2)}) collective-permute-start(f32[160,128]{1,0:T(8,128)S(1)} %get-tuple-element.41), channel_id=1, source_target_pairs={{0,12},{4,8},{8,4},{12,0},{1,13},{5,9},{9,5},{13,1},{2,14},{6,10},... | collective-permute-start | bytes 245768 | tf_op jit(solution)/shard_map/ppermute | solution.py:552
  15.4 4.2 %collective-permute-start.4 = (f32[96,128]{1,0:T(8,128)S(1)}, f32[96,128]{1,0:T(8,128)S(1)}, u32[]{:S(2)}, u32[]{:S(2)}) collective-permute-start(f32[96,128]{1,0:T(8,128)S(1)} %get-tuple-element.51), channel_id=1, source_target_pairs={{0,2},{1,3},{2,0},{3,1},{4,6},{5,7},{6,4},{7,5},{8,10},{9,11},{10,... | collective-permute-start | bytes 147464 | tf_op jit(solution)/shard_map/ppermute | solution.py:552
  17.0 2.6 %collective-permute-start.5 = (f32[96,128]{1,0:T(8,128)S(1)}, f32[96,128]{1,0:T(8,128)S(1)}, u32[]{:S(2)}, u32[]{:S(2)}) collective-permute-start(f32[96,128]{1,0:T(8,128)S(1)} %get-tuple-element.52), channel_id=1, source_target_pairs={{0,3},{1,0},{2,1},{3,2},{4,7},{5,4},{6,5},{7,6},{8,11},{9,8},{10,9... | collective-permute-start | bytes 147464 | tf_op jit(solution)/shard_map/ppermute | solution.py:552
  17.0 3.6 %collective-permute-start.3 = (f32[96,128]{1,0:T(8,128)S(1)}, f32[96,128]{1,0:T(8,128)S(1)}, u32[]{:S(2)}, u32[]{:S(2)}) collective-permute-start(f32[96,128]{1,0:T(8,128)S(1)} %get-tuple-element.45.sent_ref), channel_id=1, source_target_pairs={{0,1},{1,2},{2,3},{3,0},{4,5},{5,6},{6,7},{7,4},{8,9},{9,10},{10,1... | collective-permute-start | bytes 147464 | tf_op jit(solution)/shard_map/ppermute | solution.py:552
  17.5 3.1 %copy-start = (bf16[2,20,48,128]{3,2,1,0:T(8,128)(2,1)S(1)}, bf16[2,20,48,128]{3,2,1,0:T(8,128)(2,1)}, u32[]{:S(2)}) copy-start(bf16[2,20,48,128]{3,2,1,0:T(8,128)(2,1)} %p_ref.7) | copy-start | bytes 1474564
  21.0 6.0 %collective-permute-start.6 = (f32[5,48,128]{2,1,0:T(8,128)S(1)}, f32[5,48,128]{2,1,0:T(8,128)S(1)}, u32[]{:S(2)}, u32[]{:S(2)}) collective-permute-start(f32[5,48,128]{2,1,0:T(8,128)S(1)} %shard_map.60), channel_id=1, source_target_pairs={{0,16},{16,0},{1,17},{17,1},{2,18},{18,2},{3,19},{19,3},{4,20},{20... | collective-permute-start | bytes 368648 | tf_op jit(solution)/shard_map/ppermute | solution.py:641
  22.9 6.7 %collective-permute-start.7 = (f32[5,48,128]{2,1,0:T(8,128)S(1)}, f32[5,48,128]{2,1,0:T(8,128)S(1)}, u32[]{:S(2)}, u32[]{:S(2)}) collective-permute-start(f32[5,48,128]{2,1,0:T(8,128)S(1)} %shard_map.61), channel_id=1, source_target_pairs={{0,16},{16,0},{1,17},{17,1},{2,18},{18,2},{3,19},{19,3},{4,20},{20... | collective-permute-start | bytes 368648 | tf_op jit(solution)/shard_map/ppermute | solution.py:641
  23.9 8.3 %collective-permute-start.8 = (f32[5,48,128]{2,1,0:T(8,128)S(1)}, f32[5,48,128]{2,1,0:T(8,128)S(1)}, u32[]{:S(2)}, u32[]{:S(2)}) collective-permute-start(f32[5,48,128]{2,1,0:T(8,128)S(1)} %shard_map.62), channel_id=1, source_target_pairs={{0,16},{16,0},{1,17},{17,1},{2,18},{18,2},{3,19},{19,3},{4,20},{20... | collective-permute-start | bytes 368648 | tf_op jit(solution)/shard_map/ppermute | solution.py:641
  25.8 8.0 %collective-permute-start.9 = (f32[5,48,128]{2,1,0:T(8,128)S(1)}, f32[5,48,128]{2,1,0:T(8,128)S(1)}, u32[]{:S(2)}, u32[]{:S(2)}) collective-permute-start(f32[5,48,128]{2,1,0:T(8,128)S(1)} %shard_map.63), channel_id=1, source_target_pairs={{0,16},{16,0},{1,17},{17,1},{2,18},{18,2},{3,19},{19,3},{4,20},{20... | collective-permute-start | bytes 368648 | tf_op jit(solution)/shard_map/ppermute | solution.py:641

commit v5 on v4

--- a/solution.py
+++ b/solution.py
@@ -155,6 +155,8 @@
         for b in range(ORDER):
             packed = jnp.where(lane == a * ORDER + b, hat[a][b], packed)
     hat_ref[...] = packed
+    wide_hat = [[jnp.broadcast_to(value, full) for value in line] for line in hat]
+    over = {h: [jnp.broadcast_to(c, full) for c in power(z, h * nx)] for h in range(1, max(blocks - 1, 2))}
 
     for copy in copies[3:]:
         copy.wait()
@@ -196,16 +198,15 @@
     ends = lax.fori_loop(0, nx, onward, zeros, unroll=8)
     starts = lax.fori_loop(0, nx, backward, zeros, unroll=8)
 
-    turned = [sum(hat[a][b] * ends[b] for b in range(ORDER)) for a in range(ORDER)]
-    turned = shifted(power(z, nx), turned)
+    turned = [sum(wide_hat[a][b] * ends[b] for b in range(ORDER)) for a in range(ORDER)]
+    turned = shifted(over[1], turned)
     leaving = [starts[a] + turned[a] for a in range(ORDER)]
     for a in range(ORDER):
         end_ref[pl.ds(a * rows, rows), :] = ends[a]
     to_right, to_left = {1: ends}, {1: leaving}
     for hops in range(2, blocks):
-        over = power(z, (hops - 1) * nx)
-        to_right[hops] = shifted(over, ends)
-        to_left[hops] = shifted(over, leaving)
+        to_right[hops] = shifted(over[hops - 1], ends)
+        to_left[hops] = shifted(over[hops - 1], leaving)
     for d in range(1, blocks):
         to = target(place, d, blocks)
         reach = sorted({abs(target(i, d, blocks) - i) for i in range(blocks)})

time: 34.9 us -> 34.9 us (level)
  no operation moved by 1% of the time
where the time goes in v5:
time: 34.9 us; the launch traced here: 34.7 us
  starting transfers between devices  12.1 us (35%)
  waiting for transfers between devices  11.5 us (33%)
  Pallas kernels  10.2 us (29%)
  other arithmetic  0.89 us (3%)
    pallas_call x9, Pallas kernels, call(): pl.pallas_call(kernel, out_shape=out, in_specs=[spec() for _ in range(len...  10.2 us
    ppermute x6, starting transfers between devices, exchange(): lax.ppermute(values[d - 1], axis, [(i, to(i, d, n)) for i in range(n)])  7.8 us
    ppermute x4, waiting for transfers between devices, body(): others = [lax.ppermute(part, 'member', [(0, 1), (1, 0)]) for part in parts]  7.4 us
    ppermute x4, starting transfers between devices, body(): others = [lax.ppermute(part, 'member', [(0, 1), (1, 0)]) for part in parts]  4.29 us
    ppermute x6, waiting for transfers between devices, exchange(): lax.ppermute(values[d - 1], axis, [(i, to(i, d, n)) for i in range(n)])  4.06 us
    concatenate x1, other arithmetic, body(): return jnp.concatenate([a + b for a, b in zip(parts, others)], 0)  0.83 us
  transfers between devices with their start and end apart: 10, of which 7 were waited for; matrix products, arithmetic and copies ran while one was open for 0% of the time, Pallas kernels for 19%

profile of v5, /device:TPU:0, one launch (start us, length us, event | category | flops | bytes accessed | tf_op | source)
XLA Modules:
  0.0 34.7 jit_solution(15122486401308553321)
XLA Ops:
  0.0 2.5 %shard_map.55 = (f32[1920,128]{1,0:T(8,128)S(1)}, f32[1920,128]{1,0:T(8,128)S(1)}, f32[160,128]{1,0:T(8,128)S(1)}, f32[40,128]{1,0:T(8,128)S(1)}, f32[20,20]{1,0...) custom-call(bf16[2,20,48,128]{3,2,1,0:T(8,128)(2,1)} %p_ref.7, ...), custom_call_target="tpu_custom_call" | custom-call | flops 268435456 | bytes 3300800 | tf_op jit(solution)/shard_map/pallas_call | solution.py:534
  2.6 3.1 %collective-permute-start = (f32[160,128]{1,0:T(8,128)S(1)}, f32[160,128]{1,0:T(8,128)S(1)}, u32[]{:S(2)}, u32[]{:S(2)}) collective-permute-start(f32[160,128]{1,0:T(8,128)S(1)} %get-tuple-element.39), channel_id=1, source_target_pairs={{0,4},{4,0},{8,12},{12,8},{1,5},{5,1},{9,13},{13,9},{2,6},{6,2},{1... | collective-permute-start | bytes 245768 | tf_op jit(solution)/shard_map/ppermute | solution.py:553
  5.7 2.6 %collective-permute-start.1 = (f32[160,128]{1,0:T(8,128)S(1)}, f32[160,128]{1,0:T(8,128)S(1)}, u32[]{:S(2)}, u32[]{:S(2)}) collective-permute-start(f32[160,128]{1,0:T(8,128)S(1)} %get-tuple-element.40), channel_id=1, source_target_pairs={{0,8},{4,12},{8,0},{12,4},{1,9},{5,13},{9,1},{13,5},{2,10},{6,14},... | collective-permute-start | bytes 245768 | tf_op jit(solution)/shard_map/ppermute | solution.py:553
  8.3 0.0 collective-permute-start.2
  8.3 2.6 %shard_map.56 = (f32[128,256]{1,0:T(8,128)S(1)}, bf16[20,128,128]{2,1,0:T(8,128)(2,1)S(1)}, bf16[20,128,128]{2,1,0:T(8,128)(2,1)S(1)}, bf16[768,128]{1,0:T(8,128...) custom-call(f32[20,20]{1,0:T(8,128)S(1)} %get-tuple-element.33.e_ref, f32[1,20]{1,0:T(1,128)S(1)} %get-tuple-element.32.rx_ref, ...), custom_call_target="tpu_custom_call" | custom-call | flops 1073741824 | bytes 1726176 | tf_op jit(solution)/shard_map/pallas_call | solution.py:534
  10.9 1.1 %shard_map.57 = (f32[96,256]{1,0:T(8,128)S(1)}, f32[384,256]{1,0:T(8,128)S(1)}) custom-call(f32[1920,128]{1,0:T(8,128)S(1)} %get-tuple-element.36.z_ref, f32[128,256]{1,0:T(8,128)S(1)} %get-tuple-element.35.send_ref, f32[1,20]{1,0:T(1,128)S(1)} %get-tuple-element.32.rx_ref), custom_call_target="tpu_custom_call" | custom-call | flops 536870912 | bytes 1605712 | tf_op jit(solution)/shard_map/pallas_call | solution.py:534
  11.9 0.0 collective-permute-done.refs_0_
  11.9 2.9 %collective-permute-done.1.refs_1_ = f32[160,128]{1,0:T(8,128)S(1)} collective-permute-done((f32[160,128]{1,0:T(8,128)S(1)}, f32[160,128]{1,0:T(8,128)S(1)}, u32[]{:S(2)}, u32[]{:S(2)}) %collective-permute-start.1) | collective-permute-done | bytes 81952 | tf_op jit(solution)/shard_map/ppermute | solution.py:553
  14.9 0.0 collective-permute-done.2.refs_2_
  14.9 0.5 %shard_map.58 = (f32[320,128]{1,0:T(8,128)S(1)}, f32[96,128]{1,0:T(8,128)S(1)}, f32[96,128]{1,0:T(8,128)S(1)}, f32[96,128]{1,0:T(8,128)S(1)}) custom-call(f32[160,128]{1,0:T(8,128)S(1)} %get-tuple-element.30.end_ref, f32[40,128]{1,0:T(8,128)S(1)} %get-tuple-element.31.hat_ref, f32[1,20]{1,0:T(1,128)S(1)} %get-tuple-element.32.rx_ref, ...), custom_call_target="tpu_custom_call" | custom-call | flops 134217728 | bytes 1282128 | tf_op jit(solution)/shard_map/pallas_call | solution.py:534
  15.4 1.6 %collective-permute-start.4 = (f32[96,128]{1,0:T(8,128)S(1)}, f32[96,128]{1,0:T(8,128)S(1)}, u32[]{:S(2)}, u32[]{:S(2)}) collective-permute-start(f32[96,128]{1,0:T(8,128)S(1)} %get-tuple-element.51), channel_id=1, source_target_pairs={{0,2},{1,3},{2,0},{3,1},{4,6},{5,7},{6,4},{7,5},{8,10},{9,11},{10,... | collective-permute-start | bytes 147464 | tf_op jit(solution)/shard_map/ppermute | solution.py:553
  17.0 0.0 collective-permute-start.5
  17.0 0.5 %collective-permute-start.3 = (f32[96,128]{1,0:T(8,128)S(1)}, f32[96,128]{1,0:T(8,128)S(1)}, u32[]{:S(2)}, u32[]{:S(2)}) collective-permute-start(f32[96,128]{1,0:T(8,128)S(1)} %get-tuple-element.45.sent_ref), channel_id=1, source_target_pairs={{0,1},{1,2},{2,3},{3,0},{4,5},{5,6},{6,7},{7,4},{8,9},{9,10},{10,1... | collective-permute-start | bytes 147464 | tf_op jit(solution)/shard_map/ppermute | solution.py:553
  17.5 0.0 copy-start
  17.5 2.0 %shard_map.59 = (f32[40,48,128]{2,1,0:T(8,128)S(1)}, f32[96,128]{1,0:T(8,128)S(1)}) custom-call(f32[1920,128]{1,0:T(8,128)S(1)} %get-tuple-element.29.proj_ref, f32[320,128]{1,0:T(8,128)S(1)} %get-tuple-element.42.enter_ref, bf16[20,128,128]{2,1,0:T(8,128)(2,1)S(1)} %get-tuple-element.43.high_ref, bf16[20,128,128]{2,1,0:T(8,128)(2,1)S(1)} %get-tuple-element.44.low_ref, ...), custom_call_target="tpu_custom_call" | custom-call | flops 536870912 | bytes 3606240 | tf_op jit(solution)/shard_map/pallas_call | solution.py:534
  19.5 0.1 collective-permute-done.4.refs_1_
  19.6 0.0 collective-permute-done.5.refs_2_
  19.6 1.0 %collective-permute-done.3.refs_0_ = f32[96,128]{1,0:T(8,128)S(1)} collective-permute-done((f32[96,128]{1,0:T(8,128)S(1)}, f32[96,128]{1,0:T(8,128)S(1)}, u32[]{:S(2)}, u32[]{:S(2)}) %collective-permute-start.3) | collective-permute-done | bytes 49184 | tf_op jit(solution)/shard_map/ppermute | solution.py:553
  20.6 0.0 copy-done
  20.6 0.4 %shard_map.60 = f32[5,48,128]{2,1,0:T(8,128)S(1)} custom-call(bf16[2,20,48,128]{3,2,1,0:T(8,128)(2,1)S(1)} %copy-done, f32[40,48,128]{2,1,0:T(8,128)S(1)} %get-tuple-element.47.base_ref, f32[96,128]{1,0:T(8,128)S(1)} %get-tuple-element.48.right_ref, bf16[768,128]{1,0:T(8,128)(2,1)S(1)} %get-tuple-element.49.fix_ref, ...), custom_call_target="tpu_custom_call" | custom-call | flops 134217728 | bytes 2011136 | tf_op jit(solution)/shard_map/pallas_call | solution.py:534
  21.0 1.6 %collective-permute-start.6 = (f32[5,48,128]{2,1,0:T(8,128)S(1)}, f32[5,48,128]{2,1,0:T(8,128)S(1)}, u32[]{:S(2)}, u32[]{:S(2)}) collective-permute-start(f32[5,48,128]{2,1,0:T(8,128)S(1)} %shard_map.60), channel_id=1, source_target_pairs={{0,16},{16,0},{1,17},{17,1},{2,18},{18,2},{3,19},{19,3},{4,20},{20... | collective-permute-start | bytes 368648 | tf_op jit(solution)/shard_map/ppermute | solution.py:642
  22.6 0.4 %shard_map.61 = f32[5,48,128]{2,1,0:T(8,128)S(1)} custom-call(bf16[2,20,48,128]{3,2,1,0:T(8,128)(2,1)S(1)} %copy-done, f32[40,48,128]{2,1,0:T(8,128)S(1)} %get-tuple-element.47.base_ref, f32[96,128]{1,0:T(8,128)S(1)} %get-tuple-element.48.right_ref, bf16[768,128]{1,0:T(8,128)(2,1)S(1)} %get-tuple-element.49.fix_ref, ...), custom_call_target="tpu_custom_call" | custom-call | flops 134217728 | bytes 2011136 | tf_op jit(solution)/shard_map/pallas_call | solution.py:534
  23.0 0.6 %collective-permute-start.7 = (f32[5,48,128]{2,1,0:T(8,128)S(1)}, f32[5,48,128]{2,1,0:T(8,128)S(1)}, u32[]{:S(2)}, u32[]{:S(2)}) collective-permute-start(f32[5,48,128]{2,1,0:T(8,128)S(1)} %shard_map.61), channel_id=1, source_target_pairs={{0,16},{16,0},{1,17},{17,1},{2,18},{18,2},{3,19},{19,3},{4,20},{20... | collective-permute-start | bytes 368648 | tf_op jit(solution)/shard_map/ppermute | solution.py:642
  23.5 0.4 %shard_map.62 = f32[5,48,128]{2,1,0:T(8,128)S(1)} custom-call(bf16[2,20,48,128]{3,2,1,0:T(8,128)(2,1)S(1)} %copy-done, f32[40,48,128]{2,1,0:T(8,128)S(1)} %get-tuple-element.47.base_ref, f32[96,128]{1,0:T(8,128)S(1)} %get-tuple-element.48.right_ref, bf16[768,128]{1,0:T(8,128)(2,1)S(1)} %get-tuple-element.49.fix_ref, ...), custom_call_target="tpu_custom_call" | custom-call | flops 134217728 | bytes 2011136 | tf_op jit(solution)/shard_map/pallas_call | solution.py:534
  23.9 1.6 %collective-permute-start.8 = (f32[5,48,128]{2,1,0:T(8,128)S(1)}, f32[5,48,128]{2,1,0:T(8,128)S(1)}, u32[]{:S(2)}, u32[]{:S(2)}) collective-permute-start(f32[5,48,128]{2,1,0:T(8,128)S(1)} %shard_map.62), channel_id=1, source_target_pairs={{0,16},{16,0},{1,17},{17,1},{2,18},{18,2},{3,19},{19,3},{4,20},{20... | collective-permute-start | bytes 368648 | tf_op jit(solution)/shard_map/ppermute | solution.py:642
  25.5 0.4 %shard_map.63 = f32[5,48,128]{2,1,0:T(8,128)S(1)} custom-call(bf16[2,20,48,128]{3,2,1,0:T(8,128)(2,1)S(1)} %copy-done, f32[40,48,128]{2,1,0:T(8,128)S(1)} %get-tuple-element.47.base_ref, f32[96,128]{1,0:T(8,128)S(1)} %get-tuple-element.48.right_ref, bf16[768,128]{1,0:T(8,128)(2,1)S(1)} %get-tuple-element.49.fix_ref, ...), custom_call_target="tpu_custom_call" | custom-call | flops 134217728 | bytes 2011136 | tf_op jit(solution)/shard_map/pallas_call | solution.py:534
  25.9 0.5 %collective-permute-start.9 = (f32[5,48,128]{2,1,0:T(8,128)S(1)}, f32[5,48,128]{2,1,0:T(8,128)S(1)}, u32[]{:S(2)}, u32[]{:S(2)}) collective-permute-start(f32[5,48,128]{2,1,0:T(8,128)S(1)} %shard_map.63), channel_id=1, source_target_pairs={{0,16},{16,0},{1,17},{17,1},{2,18},{18,2},{3,19},{19,3},{4,20},{20... | collective-permute-start | bytes 368648 | tf_op jit(solution)/shard_map/ppermute | solution.py:642
  26.4 0.5 %collective-permute-done.6 = f32[5,48,128]{2,1,0:T(8,128)S(1)} collective-permute-done((f32[5,48,128]{2,1,0:T(8,128)S(1)}, f32[5,48,128]{2,1,0:T(8,128)S(1)}, u32[]{:S(2)}, u32[]{:S(2)}) %collective-permute-start.6) | collective-permute-done | bytes 122912 | tf_op jit(solution)/shard_map/ppermute | solution.py:642
  27.0 2.6 %collective-permute-done.7 = f32[5,48,128]{2,1,0:T(8,128)S(1)} collective-permute-done((f32[5,48,128]{2,1,0:T(8,128)S(1)}, f32[5,48,128]{2,1,0:T(8,128)S(1)}, u32[]{:S(2)}, u32[]{:S(2)}) %collective-permute-start.7) | collective-permute-done | bytes 122912 | tf_op jit(solution)/shard_map/ppermute | solution.py:642
  29.6 2.6 %collective-permute-done.8 = f32[5,48,128]{2,1,0:T(8,128)S(1)} collective-permute-done((f32[5,48,128]{2,1,0:T(8,128)S(1)}, f32[5,48,128]{2,1,0:T(8,128)S(1)}, u32[]{:S(2)}, u32[]{:S(2)}) %collective-permute-start.8) | collective-permute-done | bytes 122912 | tf_op jit(solution)/shard_map/ppermute | solution.py:642
  32.2 1.6 %collective-permute-done.9 = f32[5,48,128]{2,1,0:T(8,128)S(1)} collective-permute-done((f32[5,48,128]{2,1,0:T(8,128)S(1)}, f32[5,48,128]{2,1,0:T(8,128)S(1)}, u32[]{:S(2)}, u32[]{:S(2)}) %collective-permute-start.9) | collective-permute-done | bytes 122912 | tf_op jit(solution)/shard_map/ppermute | solution.py:642
  33.9 0.8 %pad_maximum_fusion = f32[20,48,128]{2,1,0:T(8,128)} fusion(f32[5,48,128]{2,1,0:T(8,128)S(1)} %add.15, f32[5,48,128]{2,1,0:T(8,128)S(1)} %add.14, f32[5,48,128]{2,1,0:T(8,128)S(1)} %add.13, f32[5,48,128]{2,1,0:T(8,128)S(1)} %add.12), kind=kLoop, calls=%fused_computation | loop fusion | flops 368640 | bytes 983040 | tf_op jit(solution)/shard_map/concatenate | solution.py:643
  (4 shorter events, 0.1 us)
Async XLA Ops:
  2.6 9.4 %collective-permute-start = (f32[160,128]{1,0:T(8,128)S(1)}, f32[160,128]{1,0:T(8,128)S(1)}, u32[]{:S(2)}, u32[]{:S(2)}) collective-permute-start(f32[160,128]{1,0:T(8,128)S(1)} %get-tuple-element.39), channel_id=1, source_target_pairs={{0,4},{4,0},{8,12},{12,8},{1,5},{5,1},{9,13},{13,9},{2,6},{6,2},{1... | collective-permute-start | bytes 245768 | tf_op jit(solution)/shard_map/ppermute | solution.py:553
  5.7 9.2 %collective-permute-start.1 = (f32[160,128]{1,0:T(8,128)S(1)}, f32[160,128]{1,0:T(8,128)S(1)}, u32[]{:S(2)}, u32[]{:S(2)}) collective-permute-start(f32[160,128]{1,0:T(8,128)S(1)} %get-tuple-element.40), channel_id=1, source_target_pairs={{0,8},{4,12},{8,0},{12,4},{1,9},{5,13},{9,1},{13,5},{2,10},{6,14},... | collective-permute-start | bytes 245768 | tf_op jit(solution)/shard_map/ppermute | solution.py:553
  8.3 6.6 %collective-permute-start.2 = (f32[160,128]{1,0:T(8,128)S(1)}, f32[160,128]{1,0:T(8,128)S(1)}, u32[]{:S(2)}, u32[]{:S(2)}) collective-permute-start(f32[160,128]{1,0:T(8,128)S(1)} %get-tuple-element.41), channel_id=1, source_target_pairs={{0,12},{4,8},{8,4},{12,0},{1,13},{5,9},{9,5},{13,1},{2,14},{6,10},... | collective-permute-start | bytes 245768 | tf_op jit(solution)/shard_map/ppermute | solution.py:553
  15.4 4.2 %collective-permute-start.4 = (f32[96,128]{1,0:T(8,128)S(1)}, f32[96,128]{1,0:T(8,128)S(1)}, u32[]{:S(2)}, u32[]{:S(2)}) collective-permute-start(f32[96,128]{1,0:T(8,128)S(1)} %get-tuple-element.51), channel_id=1, source_target_pairs={{0,2},{1,3},{2,0},{3,1},{4,6},{5,7},{6,4},{7,5},{8,10},{9,11},{10,... | collective-permute-start | bytes 147464 | tf_op jit(solution)/shard_map/ppermute | solution.py:553
  17.0 2.6 %collective-permute-start.5 = (f32[96,128]{1,0:T(8,128)S(1)}, f32[96,128]{1,0:T(8,128)S(1)}, u32[]{:S(2)}, u32[]{:S(2)}) collective-permute-start(f32[96,128]{1,0:T(8,128)S(1)} %get-tuple-element.52), channel_id=1, source_target_pairs={{0,3},{1,0},{2,1},{3,2},{4,7},{5,4},{6,5},{7,6},{8,11},{9,8},{10,9... | collective-permute-start | bytes 147464 | tf_op jit(solution)/shard_map/ppermute | solution.py:553
  17.0 3.6 %collective-permute-start.3 = (f32[96,128]{1,0:T(8,128)S(1)}, f32[96,128]{1,0:T(8,128)S(1)}, u32[]{:S(2)}, u32[]{:S(2)}) collective-permute-start(f32[96,128]{1,0:T(8,128)S(1)} %get-tuple-element.45.sent_ref), channel_id=1, source_target_pairs={{0,1},{1,2},{2,3},{3,0},{4,5},{5,6},{6,7},{7,4},{8,9},{9,10},{10,1... | collective-permute-start | bytes 147464 | tf_op jit(solution)/shard_map/ppermute | solution.py:553
  17.5 3.1 %copy-start = (bf16[2,20,48,128]{3,2,1,0:T(8,128)(2,1)S(1)}, bf16[2,20,48,128]{3,2,1,0:T(8,128)(2,1)}, u32[]{:S(2)}) copy-start(bf16[2,20,48,128]{3,2,1,0:T(8,128)(2,1)} %p_ref.7) | copy-start | bytes 1474564
  21.0 6.0 %collective-permute-start.6 = (f32[5,48,128]{2,1,0:T(8,128)S(1)}, f32[5,48,128]{2,1,0:T(8,128)S(1)}, u32[]{:S(2)}, u32[]{:S(2)}) collective-permute-start(f32[5,48,128]{2,1,0:T(8,128)S(1)} %shard_map.60), channel_id=1, source_target_pairs={{0,16},{16,0},{1,17},{17,1},{2,18},{18,2},{3,19},{19,3},{4,20},{20... | collective-permute-start | bytes 368648 | tf_op jit(solution)/shard_map/ppermute | solution.py:642
  23.0 6.6 %collective-permute-start.7 = (f32[5,48,128]{2,1,0:T(8,128)S(1)}, f32[5,48,128]{2,1,0:T(8,128)S(1)}, u32[]{:S(2)}, u32[]{:S(2)}) collective-permute-start(f32[5,48,128]{2,1,0:T(8,128)S(1)} %shard_map.61), channel_id=1, source_target_pairs={{0,16},{16,0},{1,17},{17,1},{2,18},{18,2},{3,19},{19,3},{4,20},{20... | collective-permute-start | bytes 368648 | tf_op jit(solution)/shard_map/ppermute | solution.py:642
  23.9 8.3 %collective-permute-start.8 = (f32[5,48,128]{2,1,0:T(8,128)S(1)}, f32[5,48,128]{2,1,0:T(8,128)S(1)}, u32[]{:S(2)}, u32[]{:S(2)}) collective-permute-start(f32[5,48,128]{2,1,0:T(8,128)S(1)} %shard_map.62), channel_id=1, source_target_pairs={{0,16},{16,0},{1,17},{17,1},{2,18},{18,2},{3,19},{19,3},{4,20},{20... | collective-permute-start | bytes 368648 | tf_op jit(solution)/shard_map/ppermute | solution.py:642
  25.9 8.0 %collective-permute-start.9 = (f32[5,48,128]{2,1,0:T(8,128)S(1)}, f32[5,48,128]{2,1,0:T(8,128)S(1)}, u32[]{:S(2)}, u32[]{:S(2)}) collective-permute-start(f32[5,48,128]{2,1,0:T(8,128)S(1)} %shard_map.63), channel_id=1, source_target_pairs={{0,16},{16,0},{1,17},{17,1},{2,18},{18,2},{3,19},{19,3},{4,20},{20... | collective-permute-start | bytes 368648 | tf_op jit(solution)/shard_map/ppermute | solution.py:642
